TPU v7x, 256 devices: a whole 4x4x8 slice. The times are simulated.
256 devices in a mesh: ctx: 32 (over z, x_lo, core), head: 8 (over x_hi, y).
Axes of the slice: x: 4 (x_hi: 2, x_lo: 2; x = x_hi * 2 + x_lo), y: 4, z: 8, core: 2. Of those that a mesh axis runs over, the one named last changes fastest.
Arguments:
- tokens: bfloat16 [8192, 4096], P('ctx', 'head'), may hold values from -19.8 to 19.8
- query_weight: bfloat16 [4096, 4096], P('ctx', 'head'), may hold values from -0.09375 to 0.09375
- key_weight: bfloat16 [4096, 4096], P('ctx', 'head'), may hold values from -0.09375 to 0.09375
- value_weight: bfloat16 [4096, 4096], P('ctx', 'head'), may hold values from -0.09375 to 0.09375
- output_weight: bfloat16 [4096, 4096], P('ctx', 'head'), may hold values from -0.29882812 to 0.29882812
- adapter_down: bfloat16 [3, 8, 4096], replicated, may hold values from -0.09375 to 0.09375
- adapter_up: bfloat16 [3, 8, 4096], P(None, None, 'head'), may hold values from -0.8984375 to 0.8984375
Outputs:
- attended: bfloat16 [8192, 4096], P('ctx', 'head')
All inputs are finite; a program needn't handle non-finite values.
Results may differ from a plain program's by a relative error of at most 0.012.
Values may be sent and summed in bfloat16 or wider, within the bound.
A program may use at most 64 MiB of HBM per device.

v0:
```python
import jax
import jax.numpy as jnp
from jax import lax
from jax.sharding import Mesh
from jax.sharding import PartitionSpec as P

D = 4096
HEADS = 32
GROUP_DEV = 16
CTX = ("ctx_0", "ctx_1", "ctx_2")


def in_order(tiles, dim):
    dims = list(tiles.shape[1:])
    dims[dim] *= tiles.shape[0]
    return jnp.moveaxis(tiles, 0, dim).reshape(dims)


def copy_for_each(x, axis):
    copies = jnp.broadcast_to(x, (lax.axis_size(axis), *x.shape))
    return lax.all_to_all(copies, axis, split_axis=0, concat_axis=0, tiled=True)


def collect(x, axis, dim):
    return in_order(copy_for_each(x, axis), dim)


def in_one_piece(arrays, axis, dim, along):
    ends, at = ([], 0)
    for a in arrays[:-1]:
        at += a.shape[along]
        ends.append(at)
    both = jnp.concatenate(arrays, axis=along)
    return tuple(jnp.split(lax.all_gather(both, axis, axis=dim, tiled=True), ends, axis=along))


def shifted(x, axis, by):
    peers = lax.axis_size(axis)
    return lax.ppermute(x, axis, [(i, (i + by) % peers) for i in range(peers)])


def gather_in_order(x, axes, turns):
    tiles = x
    for k in turns:
        tiles = lax.all_gather(tiles, axes[k])
    done = turns[::-1]
    back = [done.index(k) for k in range(len(axes))]
    tiles = tiles.transpose(*back, *range(len(axes), tiles.ndim))
    return tiles.reshape(-1, *x.shape)


def gathered_by_axis(x, axes, turns, dim):
    return in_order(gather_in_order(x, axes, turns), dim)


def rotary(projection, positions):
    half_dim = projection.shape[-1] // 2
    inverse_freq = 10000.0 ** (
        -(jnp.arange(half_dim, dtype=jnp.float32) * 2.0) / projection.shape[-1]
    )
    angles = positions.astype(jnp.float32)[:, None] * inverse_freq[None, :]
    cosine = jnp.cos(angles)[:, None, :]
    sine_part = jnp.sin(angles)[:, None, :]
    first_half = projection[..., :half_dim]
    second = projection[..., half_dim:]
    return jnp.concatenate(
        [first_half * cosine - second * sine_part, second * cosine + first_half * sine_part], -1
    )


def fold_rows(left_side, weight_piece):
    return jnp.dot(left_side, weight_piece, preferred_element_type=jnp.float32)


def update_block(carry, query, key_blk, value_blk, key_place, query_pos, group_size):
    row_max, denominator, running = carry
    scale = query.shape[-1] ** (-0.5)
    scores = jnp.einsum("qhd,khd->hqk", query, key_blk, preferred_element_type=jnp.float32) * scale
    allowed = ((query_pos // group_size)[:, None] == (key_place // group_size)[None, :]) & (
        key_place[None, :] <= query_pos[:, None]
    )
    scores = jnp.where(allowed[None], scores, -1e30)
    new_max = jnp.maximum(row_max, jnp.max(scores, axis=-1))
    weights = jnp.where(allowed[None], jnp.exp(scores - new_max[..., None]), 0.0)
    factor = jnp.exp(row_max - new_max)
    denominator = denominator * factor + jnp.sum(weights, axis=-1)
    running = running * factor[..., None] + jnp.einsum(
        "hqk,khd->hqd", weights.astype(jnp.bfloat16), value_blk, preferred_element_type=jnp.float32
    )
    return (new_max, denominator, running)


def per_device(
    tokens, query_weight, key_weight, value_weight, output_weight, adapter_down, adapter_up
):
    tok_rows = tokens.shape[0]
    ctx_count = lax.axis_size(CTX)
    ctx_index = lax.axis_index(CTX)
    head_count = lax.axis_size("head")
    heads_dev = HEADS // head_count
    head_dim = D // HEADS
    slab_len = tok_rows * ctx_count
    group_size = GROUP_DEV * tok_rows
    shift_span = group_size // 2
    shifted_dev = lax.axis_index("head") >= head_count // 2
    features = collect(tokens, "head", 1)
    pieces = in_one_piece((query_weight, key_weight, value_weight), CTX, 0, 1)
    projected = tuple((fold_rows(features, piece_now) for piece_now in pieces))
    low_ranks = jnp.einsum(
        "td,jrd->jtr", features, adapter_down, preferred_element_type=jnp.float32
    ).astype(jnp.bfloat16)
    local_rows = jnp.arange(tok_rows, dtype=jnp.int32)
    positions = ctx_index * tok_rows + local_rows
    full_projs = []
    for which in range(3):
        full_proj = projected[which] + 2.0 * jnp.dot(
            low_ranks[which], adapter_up[which], preferred_element_type=jnp.float32
        )
        full_projs.append(full_proj.reshape(tok_rows, heads_dev, head_dim))
    query = rotary(full_projs[0], positions).astype(jnp.bfloat16)
    key_rot = rotary(full_projs[1], positions).astype(jnp.bfloat16)
    value = full_projs[2].astype(jnp.bfloat16)
    key_value = jnp.stack([key_rot, value])
    offset = jnp.where(shifted_dev, shift_span, 0).astype(jnp.int32)
    query_pos = (positions - offset) % slab_len
    start_carry = (
        jnp.full((heads_dev, tok_rows), -1e30, jnp.float32),
        jnp.zeros((heads_dev, tok_rows), jnp.float32),
        jnp.zeros((heads_dev, tok_rows, head_dim), jnp.float32),
    )
    carry = update_block(start_carry, query, key_rot, value, query_pos, query_pos, group_size)

    def one_turn(turn, state):
        current, running_carry = state
        current = shifted(current, CTX, 1)
        source = (ctx_index - turn - 1) % ctx_count
        key_place = (source * tok_rows + local_rows - offset) % slab_len
        running_carry = update_block(
            running_carry, query, current[0], current[1], key_place, query_pos, group_size
        )
        return (current, running_carry)

    unused, carry = lax.fori_loop(0, GROUP_DEV - 1, one_turn, (key_value, carry))
    row_max, denominator, running = carry
    result = (running / denominator[..., None]).astype(jnp.bfloat16)
    result = result.transpose(1, 0, 2).reshape(tok_rows, heads_dev * head_dim)
    merged = collect(result, "head", 1)
    attended = fold_rows(merged, gathered_by_axis(output_weight, CTX, (1, 0, 2), 0))
    return attended.astype(jnp.bfloat16)


def solution(mesh):
    split = Mesh(
        mesh.devices.reshape(8, 2, 2, mesh.shape["head"]), ("ctx_0", "ctx_1", "ctx_2", "head")
    )
    placed = (
        P(CTX, "head"),
        P(CTX, "head"),
        P(CTX, "head"),
        P(CTX, "head"),
        P(CTX, "head"),
        P(),
        P(None, None, "head"),
    )
    return jax.shard_map(
        per_device, mesh=split, in_specs=placed, out_specs=P(CTX, "head"), check_vma=False
    )
```

profile of v0, /device:TPU:24, one launch (start us, length us, event | category | flops | bytes accessed | tf_op | source)
XLA Modules:
  0.0 373.9 jit_solution(8899867095104405747)
XLA Ops:
  6.5 7.6 %all-gather = bf16[256,512]{1,0:T(8,128)(2,1)} all-gather(bf16[128,512]{1,0:T(8,128)(2,1)} %param.13), channel_id=2, replica_groups=mesh['ctx_0'=8,'ctx_1'=2,'ctx_2'=2,'head'=8] {'ctx_1'}, dimensions={0}, use_global_device_ids=true | all-gather | bytes 393216 | tf_op jit(solution)/shard_map/all_gather | solution.py:45
  18.6 6.9 %all-to-all-start = ((bf16[8,256,512]{2,1,0:T(8,128)(2,1)}), bf16[8,256,512]{2,1,0:T(8,128)(2,1)S(1)}, u32[]{:S(2)}, u32[]{:S(2)}) async-start(bf16[8,256,512]{2,1,0:T(8,128)(2,1)} %broadcast_in_dim.115), calls=%async_computation | async-start | bytes 4194304 | tf_op jit(solution)/shard_map/all_to_all | solution.py:21
  26.8 23.9 %all-to-all-done = bf16[8,256,512]{2,1,0:T(8,128)(2,1)S(1)} async-done(((bf16[8,256,512]{2,1,0:T(8,128)(2,1)}), bf16[8,256,512]{2,1,0:T(8,128)(2,1)S(1)}, u32[]{:S(2)}, u32[]{:S(2)}) %all-to-all-start) | async-done | bytes 2097184 | tf_op jit(solution)/shard_map/all_to_all | solution.py:21
  58.4 80.1 %all-gather.7.cloned.1.call-done = bf16[4096,1536]{1,0:T(8,128)(2,1)} async-done(((bf16[128,1536]{1,0:T(8,128)(2,1)}), bf16[4096,1536]{1,0:T(8,128)(2,1)}) %all-gather.7.cloned.1.call-update) | async-done | bytes 12582928 | tf_op jit(solution)/shard_map/all_gather | solution.py:34
  157.3 179.5 %while.24 = (s32[]{:T(128)}, bf16[2,256,4,128]{3,1,2,0:T(8,128)(2,1)S(1)}, f32[4,256]{1,0:T(4,128)S(1)}, f32[4,256]{1,0:T(4,128)S(1)}, f32[4,256,128]{2,1,0:T(8,...) while((s32[]{:T(128)}, ...), condition=%wide.region_5.6_spmd.clone.clone, body=%wide.region_2.5_spmd.clone.clone.sunk | while | flops 137065488 | bytes 8465262 | solution.py:143
  158.0 10.2 %collective-permute-done = bf16[2,256,4,128]{3,1,2,0:T(8,128)(2,1)S(1)} collective-permute-done((bf16[2,256,4,128]{3,1,2,0:T(8,128)(2,1)S(1)}, bf16[2,256,4,128]{3,1,2,0:T(8,128)(2,1)S(1)}, u32[]{:S(2)}, u32[]{:S(2)}) %collective-permute-start) | collective-permute-done | bytes 524320 | tf_op jit(solution)/shard_map/while/body/eval_jaxpr/ppermute | solution.py:39
  169.7 10.4 %collective-permute-done = bf16[2,256,4,128]{3,1,2,0:T(8,128)(2,1)S(1)} collective-permute-done((bf16[2,256,4,128]{3,1,2,0:T(8,128)(2,1)S(1)}, bf16[2,256,4,128]{3,1,2,0:T(8,128)(2,1)S(1)}, u32[]{:S(2)}, u32[]{:S(2)}) %collective-permute-start) | collective-permute-done | bytes 524320 | tf_op jit(solution)/shard_map/while/body/eval_jaxpr/ppermute | solution.py:39
  181.6 10.4 %collective-permute-done = bf16[2,256,4,128]{3,1,2,0:T(8,128)(2,1)S(1)} collective-permute-done((bf16[2,256,4,128]{3,1,2,0:T(8,128)(2,1)S(1)}, bf16[2,256,4,128]{3,1,2,0:T(8,128)(2,1)S(1)}, u32[]{:S(2)}, u32[]{:S(2)}) %collective-permute-start) | collective-permute-done | bytes 524320 | tf_op jit(solution)/shard_map/while/body/eval_jaxpr/ppermute | solution.py:39
  193.6 10.4 %collective-permute-done = bf16[2,256,4,128]{3,1,2,0:T(8,128)(2,1)S(1)} collective-permute-done((bf16[2,256,4,128]{3,1,2,0:T(8,128)(2,1)S(1)}, bf16[2,256,4,128]{3,1,2,0:T(8,128)(2,1)S(1)}, u32[]{:S(2)}, u32[]{:S(2)}) %collective-permute-start) | collective-permute-done | bytes 524320 | tf_op jit(solution)/shard_map/while/body/eval_jaxpr/ppermute | solution.py:39
  205.6 10.4 %collective-permute-done = bf16[2,256,4,128]{3,1,2,0:T(8,128)(2,1)S(1)} collective-permute-done((bf16[2,256,4,128]{3,1,2,0:T(8,128)(2,1)S(1)}, bf16[2,256,4,128]{3,1,2,0:T(8,128)(2,1)S(1)}, u32[]{:S(2)}, u32[]{:S(2)}) %collective-permute-start) | collective-permute-done | bytes 524320 | tf_op jit(solution)/shard_map/while/body/eval_jaxpr/ppermute | solution.py:39
  217.5 10.4 %collective-permute-done = bf16[2,256,4,128]{3,1,2,0:T(8,128)(2,1)S(1)} collective-permute-done((bf16[2,256,4,128]{3,1,2,0:T(8,128)(2,1)S(1)}, bf16[2,256,4,128]{3,1,2,0:T(8,128)(2,1)S(1)}, u32[]{:S(2)}, u32[]{:S(2)}) %collective-permute-start) | collective-permute-done | bytes 524320 | tf_op jit(solution)/shard_map/while/body/eval_jaxpr/ppermute | solution.py:39
  229.5 10.4 %collective-permute-done = bf16[2,256,4,128]{3,1,2,0:T(8,128)(2,1)S(1)} collective-permute-done((bf16[2,256,4,128]{3,1,2,0:T(8,128)(2,1)S(1)}, bf16[2,256,4,128]{3,1,2,0:T(8,128)(2,1)S(1)}, u32[]{:S(2)}, u32[]{:S(2)}) %collective-permute-start) | collective-permute-done | bytes 524320 | tf_op jit(solution)/shard_map/while/body/eval_jaxpr/ppermute | solution.py:39
  241.4 10.4 %collective-permute-done = bf16[2,256,4,128]{3,1,2,0:T(8,128)(2,1)S(1)} collective-permute-done((bf16[2,256,4,128]{3,1,2,0:T(8,128)(2,1)S(1)}, bf16[2,256,4,128]{3,1,2,0:T(8,128)(2,1)S(1)}, u32[]{:S(2)}, u32[]{:S(2)}) %collective-permute-start) | collective-permute-done | bytes 524320 | tf_op jit(solution)/shard_map/while/body/eval_jaxpr/ppermute | solution.py:39
  253.4 10.4 %collective-permute-done = bf16[2,256,4,128]{3,1,2,0:T(8,128)(2,1)S(1)} collective-permute-done((bf16[2,256,4,128]{3,1,2,0:T(8,128)(2,1)S(1)}, bf16[2,256,4,128]{3,1,2,0:T(8,128)(2,1)S(1)}, u32[]{:S(2)}, u32[]{:S(2)}) %collective-permute-start) | collective-permute-done | bytes 524320 | tf_op jit(solution)/shard_map/while/body/eval_jaxpr/ppermute | solution.py:39
  265.3 10.4 %collective-permute-done = bf16[2,256,4,128]{3,1,2,0:T(8,128)(2,1)S(1)} collective-permute-done((bf16[2,256,4,128]{3,1,2,0:T(8,128)(2,1)S(1)}, bf16[2,256,4,128]{3,1,2,0:T(8,128)(2,1)S(1)}, u32[]{:S(2)}, u32[]{:S(2)}) %collective-permute-start) | collective-permute-done | bytes 524320 | tf_op jit(solution)/shard_map/while/body/eval_jaxpr/ppermute | solution.py:39
  277.3 10.4 %collective-permute-done = bf16[2,256,4,128]{3,1,2,0:T(8,128)(2,1)S(1)} collective-permute-done((bf16[2,256,4,128]{3,1,2,0:T(8,128)(2,1)S(1)}, bf16[2,256,4,128]{3,1,2,0:T(8,128)(2,1)S(1)}, u32[]{:S(2)}, u32[]{:S(2)}) %collective-permute-start) | collective-permute-done | bytes 524320 | tf_op jit(solution)/shard_map/while/body/eval_jaxpr/ppermute | solution.py:39
  289.3 10.4 %collective-permute-done = bf16[2,256,4,128]{3,1,2,0:T(8,128)(2,1)S(1)} collective-permute-done((bf16[2,256,4,128]{3,1,2,0:T(8,128)(2,1)S(1)}, bf16[2,256,4,128]{3,1,2,0:T(8,128)(2,1)S(1)}, u32[]{:S(2)}, u32[]{:S(2)}) %collective-permute-start) | collective-permute-done | bytes 524320 | tf_op jit(solution)/shard_map/while/body/eval_jaxpr/ppermute | solution.py:39
  301.2 10.4 %collective-permute-done = bf16[2,256,4,128]{3,1,2,0:T(8,128)(2,1)S(1)} collective-permute-done((bf16[2,256,4,128]{3,1,2,0:T(8,128)(2,1)S(1)}, bf16[2,256,4,128]{3,1,2,0:T(8,128)(2,1)S(1)}, u32[]{:S(2)}, u32[]{:S(2)}) %collective-permute-start) | collective-permute-done | bytes 524320 | tf_op jit(solution)/shard_map/while/body/eval_jaxpr/ppermute | solution.py:39
  313.2 10.4 %collective-permute-done = bf16[2,256,4,128]{3,1,2,0:T(8,128)(2,1)S(1)} collective-permute-done((bf16[2,256,4,128]{3,1,2,0:T(8,128)(2,1)S(1)}, bf16[2,256,4,128]{3,1,2,0:T(8,128)(2,1)S(1)}, u32[]{:S(2)}, u32[]{:S(2)}) %collective-permute-start) | collective-permute-done | bytes 524320 | tf_op jit(solution)/shard_map/while/body/eval_jaxpr/ppermute | solution.py:39
  325.1 10.5 %collective-permute-done = bf16[2,256,4,128]{3,1,2,0:T(8,128)(2,1)S(1)} collective-permute-done((bf16[2,256,4,128]{3,1,2,0:T(8,128)(2,1)S(1)}, bf16[2,256,4,128]{3,1,2,0:T(8,128)(2,1)S(1)}, u32[]{:S(2)}, u32[]{:S(2)}) %collective-permute-start) | collective-permute-done | bytes 524320 | tf_op jit(solution)/shard_map/while/body/eval_jaxpr/ppermute | solution.py:39
  338.6 7.2 %all-to-all-start.1 = ((bf16[8,256,512]{1,2,0:T(8,128)(2,1)}), bf16[8,256,512]{1,2,0:T(8,128)(2,1)S(1)}, u32[]{:S(2)}, u32[]{:S(2)}) async-start(bf16[8,256,512]{1,2,0:T(8,128)(2,1)} %broadcast_in_dim.121), calls=%async_computation.1 | async-start | bytes 4194304 | tf_op jit(solution)/shard_map/all_to_all | solution.py:21
  345.8 4.6 %copy.57 = bf16[8,2,2,128,512]{4,3,2,1,0:T(8,128)(2,1)} copy(bf16[8,2,2,128,512]{4,3,1,0,2:T(8,128)(2,1)} %bitcast.76) | data formatting | bytes 8388608 | tf_op jit(solution)/shard_map/transpose | solution.py:48
  350.4 12.9 %all-to-all-done.1 = bf16[8,256,512]{1,2,0:T(8,128)(2,1)S(1)} async-done(((bf16[8,256,512]{1,2,0:T(8,128)(2,1)}), bf16[8,256,512]{1,2,0:T(8,128)(2,1)S(1)}, u32[]{:S(2)}, u32[]{:S(2)}) %all-to-all-start.1) | async-done | bytes 2097184 | tf_op jit(solution)/shard_map/all_to_all | solution.py:21
  363.2 4.2 %convolution_convert_fusion = bf16[256,512]{1,0:T(8,128)(2,1)} fusion(bf16[256,4096]{0,1:T(8,128)(2,1)S(1)} %bitcast.86, bf16[4096,512]{1,0:T(8,128)(2,1)} %bitcast.77), kind=kOutput, calls=%fused_computation.61 | convolution fusion | flops 1073872896 | bytes 6553600 | tf_op jit(solution)/shard_map/dot_general | solution.py:72
  (248 shorter events, 55.5 us)
Async XLA Ops:
  6.5 51.2 %copy-start = (bf16[3,8,4096]{2,1,0:T(8,128)(2,1)S(1)}, bf16[3,8,4096]{2,1,0:T(8,128)(2,1)}, u32[]{:S(2)}) copy-start(bf16[3,8,4096]{2,1,0:T(8,128)(2,1)} %param.14) | copy-start | bytes 589828
  6.5 51.9 %all-gather.9.cloned.1.call-start = ((), (), s32[]{:S(2)}) async-start(), calls=%async_computation.3 | async-start | bytes 2359296 | tf_op jit(solution)/shard_map/all_gather | solution.py:45
  14.2 124.3 %all-gather.7.cloned.1.call-start = ((), (), s32[]{:S(2)}) async-start(), calls=%async_computation.2 | async-start | bytes 12976128 | tf_op jit(solution)/shard_map/all_gather | solution.py:34
  18.6 32.1 %all-to-all-start = ((bf16[8,256,512]{2,1,0:T(8,128)(2,1)}), bf16[8,256,512]{2,1,0:T(8,128)(2,1)S(1)}, u32[]{:S(2)}, u32[]{:S(2)}) async-start(bf16[8,256,512]{2,1,0:T(8,128)(2,1)} %broadcast_in_dim.115), calls=%async_computation | async-start | bytes 4194304 | tf_op jit(solution)/shard_map/all_to_all | solution.py:21
  25.4 320.3 %all-gather.11.cloned.1.call-start = ((), (), s32[]{:S(2)}) async-start(), calls=%async_computation.4 | async-start | bytes 6291456 | tf_op jit(solution)/shard_map/all_gather | solution.py:45
  58.4 80.1 %copy-start.1 = (bf16[8,32,8,512]{3,2,0,1:T(8,128)(2,1)S(1)}, bf16[8,32,8,512]{3,2,0,1:T(8,128)(2,1)}, u32[]{:S(2)}) copy-start(bf16[8,32,8,512]{3,2,0,1:T(8,128)(2,1)} %copy.68) | copy-start | bytes 6291460
  138.5 3.5 copy-start.4
  154.1 1.5 copy-start.2
  157.4 10.8 %collective-permute-start = (bf16[2,256,4,128]{3,1,2,0:T(8,128)(2,1)S(1)}, bf16[2,256,4,128]{3,1,2,0:T(8,128)(2,1)S(1)}, u32[]{:S(2)}, u32[]{:S(2)}) collective-permute-start(bf16[2,256,4,128]{3,1,2,0:T(8,128)(2,1)S(1)} %get-tuple-element.504), channel_id=1, source_target_pairs={{0,8},{8,16},{16,24},{24,32},{32,40},{40,48},{48,56},{56,64},{64,7... | collective-permute-start | bytes 1572872 | tf_op jit(solution)/shard_map/while/body/eval_jaxpr/ppermute | solution.py:39
  169.3 10.8 %collective-permute-start = (bf16[2,256,4,128]{3,1,2,0:T(8,128)(2,1)S(1)}, bf16[2,256,4,128]{3,1,2,0:T(8,128)(2,1)S(1)}, u32[]{:S(2)}, u32[]{:S(2)}) collective-permute-start(bf16[2,256,4,128]{3,1,2,0:T(8,128)(2,1)S(1)} %get-tuple-element.504), channel_id=1, source_target_pairs={{0,8},{8,16},{16,24},{24,32},{32,40},{40,48},{48,56},{56,64},{64,7... | collective-permute-start | bytes 1572872 | tf_op jit(solution)/shard_map/while/body/eval_jaxpr/ppermute | solution.py:39
  181.3 10.8 %collective-permute-start = (bf16[2,256,4,128]{3,1,2,0:T(8,128)(2,1)S(1)}, bf16[2,256,4,128]{3,1,2,0:T(8,128)(2,1)S(1)}, u32[]{:S(2)}, u32[]{:S(2)}) collective-permute-start(bf16[2,256,4,128]{3,1,2,0:T(8,128)(2,1)S(1)} %get-tuple-element.504), channel_id=1, source_target_pairs={{0,8},{8,16},{16,24},{24,32},{32,40},{40,48},{48,56},{56,64},{64,7... | collective-permute-start | bytes 1572872 | tf_op jit(solution)/shard_map/while/body/eval_jaxpr/ppermute | solution.py:39
  193.2 10.8 %collective-permute-start = (bf16[2,256,4,128]{3,1,2,0:T(8,128)(2,1)S(1)}, bf16[2,256,4,128]{3,1,2,0:T(8,128)(2,1)S(1)}, u32[]{:S(2)}, u32[]{:S(2)}) collective-permute-start(bf16[2,256,4,128]{3,1,2,0:T(8,128)(2,1)S(1)} %get-tuple-element.504), channel_id=1, source_target_pairs={{0,8},{8,16},{16,24},{24,32},{32,40},{40,48},{48,56},{56,64},{64,7... | collective-permute-start | bytes 1572872 | tf_op jit(solution)/shard_map/while/body/eval_jaxpr/ppermute | solution.py:39
  205.2 10.8 %collective-permute-start = (bf16[2,256,4,128]{3,1,2,0:T(8,128)(2,1)S(1)}, bf16[2,256,4,128]{3,1,2,0:T(8,128)(2,1)S(1)}, u32[]{:S(2)}, u32[]{:S(2)}) collective-permute-start(bf16[2,256,4,128]{3,1,2,0:T(8,128)(2,1)S(1)} %get-tuple-element.504), channel_id=1, source_target_pairs={{0,8},{8,16},{16,24},{24,32},{32,40},{40,48},{48,56},{56,64},{64,7... | collective-permute-start | bytes 1572872 | tf_op jit(solution)/shard_map/while/body/eval_jaxpr/ppermute | solution.py:39
  217.2 10.8 %collective-permute-start = (bf16[2,256,4,128]{3,1,2,0:T(8,128)(2,1)S(1)}, bf16[2,256,4,128]{3,1,2,0:T(8,128)(2,1)S(1)}, u32[]{:S(2)}, u32[]{:S(2)}) collective-permute-start(bf16[2,256,4,128]{3,1,2,0:T(8,128)(2,1)S(1)} %get-tuple-element.504), channel_id=1, source_target_pairs={{0,8},{8,16},{16,24},{24,32},{32,40},{40,48},{48,56},{56,64},{64,7... | collective-permute-start | bytes 1572872 | tf_op jit(solution)/shard_map/while/body/eval_jaxpr/ppermute | solution.py:39
  229.1 10.8 %collective-permute-start = (bf16[2,256,4,128]{3,1,2,0:T(8,128)(2,1)S(1)}, bf16[2,256,4,128]{3,1,2,0:T(8,128)(2,1)S(1)}, u32[]{:S(2)}, u32[]{:S(2)}) collective-permute-start(bf16[2,256,4,128]{3,1,2,0:T(8,128)(2,1)S(1)} %get-tuple-element.504), channel_id=1, source_target_pairs={{0,8},{8,16},{16,24},{24,32},{32,40},{40,48},{48,56},{56,64},{64,7... | collective-permute-start | bytes 1572872 | tf_op jit(solution)/shard_map/while/body/eval_jaxpr/ppermute | solution.py:39
  241.1 10.8 %collective-permute-start = (bf16[2,256,4,128]{3,1,2,0:T(8,128)(2,1)S(1)}, bf16[2,256,4,128]{3,1,2,0:T(8,128)(2,1)S(1)}, u32[]{:S(2)}, u32[]{:S(2)}) collective-permute-start(bf16[2,256,4,128]{3,1,2,0:T(8,128)(2,1)S(1)} %get-tuple-element.504), channel_id=1, source_target_pairs={{0,8},{8,16},{16,24},{24,32},{32,40},{40,48},{48,56},{56,64},{64,7... | collective-permute-start | bytes 1572872 | tf_op jit(solution)/shard_map/while/body/eval_jaxpr/ppermute | solution.py:39
  253.0 10.8 %collective-permute-start = (bf16[2,256,4,128]{3,1,2,0:T(8,128)(2,1)S(1)}, bf16[2,256,4,128]{3,1,2,0:T(8,128)(2,1)S(1)}, u32[]{:S(2)}, u32[]{:S(2)}) collective-permute-start(bf16[2,256,4,128]{3,1,2,0:T(8,128)(2,1)S(1)} %get-tuple-element.504), channel_id=1, source_target_pairs={{0,8},{8,16},{16,24},{24,32},{32,40},{40,48},{48,56},{56,64},{64,7... | collective-permute-start | bytes 1572872 | tf_op jit(solution)/shard_map/while/body/eval_jaxpr/ppermute | solution.py:39
  265.0 10.8 %collective-permute-start = (bf16[2,256,4,128]{3,1,2,0:T(8,128)(2,1)S(1)}, bf16[2,256,4,128]{3,1,2,0:T(8,128)(2,1)S(1)}, u32[]{:S(2)}, u32[]{:S(2)}) collective-permute-start(bf16[2,256,4,128]{3,1,2,0:T(8,128)(2,1)S(1)} %get-tuple-element.504), channel_id=1, source_target_pairs={{0,8},{8,16},{16,24},{24,32},{32,40},{40,48},{48,56},{56,64},{64,7... | collective-permute-start | bytes 1572872 | tf_op jit(solution)/shard_map/while/body/eval_jaxpr/ppermute | solution.py:39
  276.9 10.8 %collective-permute-start = (bf16[2,256,4,128]{3,1,2,0:T(8,128)(2,1)S(1)}, bf16[2,256,4,128]{3,1,2,0:T(8,128)(2,1)S(1)}, u32[]{:S(2)}, u32[]{:S(2)}) collective-permute-start(bf16[2,256,4,128]{3,1,2,0:T(8,128)(2,1)S(1)} %get-tuple-element.504), channel_id=1, source_target_pairs={{0,8},{8,16},{16,24},{24,32},{32,40},{40,48},{48,56},{56,64},{64,7... | collective-permute-start | bytes 1572872 | tf_op jit(solution)/shard_map/while/body/eval_jaxpr/ppermute | solution.py:39
  288.9 10.8 %collective-permute-start = (bf16[2,256,4,128]{3,1,2,0:T(8,128)(2,1)S(1)}, bf16[2,256,4,128]{3,1,2,0:T(8,128)(2,1)S(1)}, u32[]{:S(2)}, u32[]{:S(2)}) collective-permute-start(bf16[2,256,4,128]{3,1,2,0:T(8,128)(2,1)S(1)} %get-tuple-element.504), channel_id=1, source_target_pairs={{0,8},{8,16},{16,24},{24,32},{32,40},{40,48},{48,56},{56,64},{64,7... | collective-permute-start | bytes 1572872 | tf_op jit(solution)/shard_map/while/body/eval_jaxpr/ppermute | solution.py:39
  300.9 10.8 %collective-permute-start = (bf16[2,256,4,128]{3,1,2,0:T(8,128)(2,1)S(1)}, bf16[2,256,4,128]{3,1,2,0:T(8,128)(2,1)S(1)}, u32[]{:S(2)}, u32[]{:S(2)}) collective-permute-start(bf16[2,256,4,128]{3,1,2,0:T(8,128)(2,1)S(1)} %get-tuple-element.504), channel_id=1, source_target_pairs={{0,8},{8,16},{16,24},{24,32},{32,40},{40,48},{48,56},{56,64},{64,7... | collective-permute-start | bytes 1572872 | tf_op jit(solution)/shard_map/while/body/eval_jaxpr/ppermute | solution.py:39
  312.8 10.8 %collective-permute-start = (bf16[2,256,4,128]{3,1,2,0:T(8,128)(2,1)S(1)}, bf16[2,256,4,128]{3,1,2,0:T(8,128)(2,1)S(1)}, u32[]{:S(2)}, u32[]{:S(2)}) collective-permute-start(bf16[2,256,4,128]{3,1,2,0:T(8,128)(2,1)S(1)} %get-tuple-element.504), channel_id=1, source_target_pairs={{0,8},{8,16},{16,24},{24,32},{32,40},{40,48},{48,56},{56,64},{64,7... | collective-permute-start | bytes 1572872 | tf_op jit(solution)/shard_map/while/body/eval_jaxpr/ppermute | solution.py:39
  324.8 10.9 %collective-permute-start = (bf16[2,256,4,128]{3,1,2,0:T(8,128)(2,1)S(1)}, bf16[2,256,4,128]{3,1,2,0:T(8,128)(2,1)S(1)}, u32[]{:S(2)}, u32[]{:S(2)}) collective-permute-start(bf16[2,256,4,128]{3,1,2,0:T(8,128)(2,1)S(1)} %get-tuple-element.504), channel_id=1, source_target_pairs={{0,8},{8,16},{16,24},{24,32},{32,40},{40,48},{48,56},{56,64},{64,7... | collective-permute-start | bytes 1572872 | tf_op jit(solution)/shard_map/while/body/eval_jaxpr/ppermute | solution.py:39
  338.6 24.7 %all-to-all-start.1 = ((bf16[8,256,512]{1,2,0:T(8,128)(2,1)}), bf16[8,256,512]{1,2,0:T(8,128)(2,1)S(1)}, u32[]{:S(2)}, u32[]{:S(2)}) async-start(bf16[8,256,512]{1,2,0:T(8,128)(2,1)} %broadcast_in_dim.121), calls=%async_computation.1 | async-start | bytes 4194304 | tf_op jit(solution)/shard_map/all_to_all | solution.py:21
  (1 other events, 1.5 us)
Sparse Core Ops, SparseCore 0:
  14.3 43.7 all-gather.8
  60.0 78.4 all-gather.6
  140.3 19.5 all-gather.10
where the time goes:
time: 374 us
  waiting for transfers between devices  273 us (73%)
  matrix products  30.7 us (8%)
  local copies, waits for them, and re-layouts  20.9 us (6%)
  starting transfers between devices  15.6 us (4%)
  between operations  13.3 us (4%)
  other arithmetic  10.9 us (3%)
  blocking collectives  7.64 us (2%)
    ppermute x15, waiting for transfers between devices, shifted(): return lax.ppermute(x, axis, [(i, (i + by) % peers) for i in range(peers)])  156 us
    all_gather x1, waiting for transfers between devices, in_one_piece(): lax.all_gather(both, axis, axis=dim, tiled=True)  80.1 us
    all_to_all x2, waiting for transfers between devices, copy_for_each(): return lax.all_to_all(copies, axis, split_axis=0, concat_axis=0, tiled=True)  36.7 us
    dot_general x4, matrix products, fold_rows(): return jnp.dot(left_side, weight_piece, preferred_element_type=jnp.float32)  15 us
    all_to_all x2, starting transfers between devices, copy_for_each(): return lax.all_to_all(copies, axis, split_axis=0, concat_axis=0, tiled=True)  14.1 us
    dot_general x16, matrix products, update_block(): jnp.einsum('hqk,khd->hqd', weights.astype(jnp.bfloat16), value_blk, prefe...  8.27 us
    all_gather x1, blocking collectives, gather_in_order(): tiles = lax.all_gather(tiles, axes[k])  7.64 us
  transfers between devices with their start and end apart: 20, of which 18 were waited for; matrix products, arithmetic and copies ran while one was open for 16% of the time, Pallas kernels for 0%

commit v1 on v0

v1 whole, which is shorter than its diff:
```python
import functools

import jax
import jax.numpy as jnp
from jax import lax
from jax.experimental import pallas as pl
from jax.experimental.pallas import tpu as pltpu
from jax.sharding import PartitionSpec as P

D = 4096
HEADS = 32
HEAD = 128
TOK = 256
MESH = pl.DeviceIdType.MESH
BF16 = jnp.bfloat16
F32 = jnp.float32


class Place:
    def __init__(self):
        c = lax.axis_index("ctx")
        h = lax.axis_index("head")
        self.z = lax.div(c, 4)
        self.xl = lax.rem(lax.div(c, 2), 2)
        self.k = lax.rem(c, 2)
        self.xh = lax.div(h, 4)
        self.y = lax.rem(h, 4)
        self.x = self.xh * 2 + self.xl
        self.h = h
        self.sigma = 1 - 2 * self.k

    def at(self, z=None, x=None, y=None, k=None):
        z = self.z if z is None else z
        x = self.x if x is None else x
        y = self.y if y is None else y
        k = self.k if k is None else k
        return (z * 4 + lax.rem(x, 2) * 2 + k, lax.div(x, 2) * 4 + y)

    def to_z(self, step):
        return self.at(z=lax.rem(self.z + 8 + step, 8))

    def to_x(self, step):
        return self.at(x=lax.rem(self.x + 4 + step, 4))

    def to_y(self, step):
        return self.at(y=lax.rem(self.y + 4 + step, 4))

    def sibling(self):
        return self.at(k=1 - self.k)

    def partner(self):
        return self.at(x=self.xh * 2 + 1 - self.xl)


def greet(devices):
    barrier = pltpu.get_barrier_semaphore()
    for device in devices:
        pl.semaphore_signal(barrier, inc=1, device_id=device, device_id_type=MESH)
    pl.semaphore_wait(barrier, len(devices))


class Sends:
    def __init__(self, send_sem, recv_sem):
        self.send_sem, self.recv_sem, self.count, self.open = send_sem, recv_sem, 0, []

    def slot(self):
        self.count += 1
        return self.count - 1

    def start(self, src, dst, device, slot):
        copy = pltpu.make_async_remote_copy(
            src_ref=src,
            dst_ref=dst,
            send_sem=self.send_sem.at[slot],
            recv_sem=self.recv_sem.at[slot],
            device_id=device,
            device_id_type=MESH,
        )
        copy.start()
        self.open.append(copy)
        return copy

    def finish(self):
        for copy in self.open:
            copy.wait_send()


class Ring4:
    def __init__(self, sends, me, sigma, to, block):
        self.sends, self.me, self.sigma, self.to, self.block = sends, me, sigma, to, block

    def place(self, step):
        return self.block(lax.rem(self.me + 4 + step * self.sigma, 4))

    def start(self):
        own = self.place(0)
        self.ahead = self.sends.start(own, own, self.to(self.sigma), self.sends.slot())
        self.back = self.sends.start(own, own, self.to(-self.sigma), self.sends.slot())

    def forward(self):
        self.ahead.wait_recv()
        block = self.place(-1)
        self.far = self.sends.start(block, block, self.to(self.sigma), self.sends.slot())

    def wait_back(self):
        self.back.wait_recv()

    def wait_far(self):
        self.far.wait_recv()


class PlaneGather:
    def __init__(self, sends, me, block):
        self.me, self.sends = me, sends
        s = me.sigma
        self.first = [
            Ring4(sends, me.x, s, me.to_x, lambda a: block(0, a, me.y)),
            Ring4(sends, me.y, s, me.to_y, lambda a: block(1, me.x, a)),
        ]
        self.second = [[], []]
        for step in (0, -1, 1, -2):
            x = lax.rem(me.x + 4 + step * s, 4)
            y = lax.rem(me.y + 4 + step * s, 4)
            self.second[0].append(Ring4(sends, me.y, s, me.to_y, lambda a, x=x: block(0, x, a)))
            self.second[1].append(Ring4(sends, me.x, s, me.to_x, lambda a, y=y: block(1, a, y)))

    def events(self):
        def start():
            for half in (0, 1):
                self.first[half].start()
            for half in (0, 1):
                self.second[half][0].start()

        def ahead():
            for half in (0, 1):
                self.first[half].forward()
                self.second[half][1].start()

        def back():
            for half in (0, 1):
                self.first[half].wait_back()
                self.second[half][2].start()

        def far():
            for half in (0, 1):
                self.first[half].wait_far()
                self.second[half][3].start()

        def second(i):
            def step():
                for half in (0, 1):
                    self.second[half][i].forward()

            return step

        def finish():
            for half in (0, 1):
                for ring in self.second[half]:
                    ring.wait_back()
                    ring.wait_far()

        return [start, ahead, back, second(0), far, second(1), second(2), second(3), finish]


class RingZ:
    def __init__(self, sends, me, block):
        self.sends, self.me, self.block = sends, me, block
        self.ahead, self.back, self.shared = {}, {}, {}

    def place(self, step, k):
        return self.block(lax.rem(self.me.z + 8 + step, 8), k)

    def share(self, key, step):
        block = self.place(step, self.me.k)
        self.shared[key] = self.sends.start(block, block, self.me.sibling(), self.sends.slot())

    def start(self):
        me, own = self.me, self.place(0, self.me.k)
        self.ahead[1] = self.sends.start(own, own, me.to_z(me.sigma), self.sends.slot())
        self.back[1] = self.sends.start(own, own, me.to_z(-me.sigma), self.sends.slot())
        self.share("own", 0)

    def take_ahead(self, s):
        me = self.me
        self.ahead[s].wait_recv()
        if s < 4:
            block = self.place(-s * me.sigma, me.k)
            self.ahead[s + 1] = self.sends.start(block, block, me.to_z(me.sigma), self.sends.slot())
        self.share(("a", s), -s * me.sigma)

    def take_back(self, s):
        me = self.me
        self.back[s].wait_recv()
        if s < 3:
            block = self.place(s * me.sigma, me.k)
            self.back[s + 1] = self.sends.start(block, block, me.to_z(-me.sigma), self.sends.slot())
        self.share(("b", s), s * me.sigma)

    def wait_shared(self, key):
        self.shared[key].wait_recv()


def all_neighbours(me):
    return [
        me.to_z(1),
        me.to_z(-1),
        me.to_x(1),
        me.to_x(-1),
        me.to_y(1),
        me.to_y(-1),
        me.sibling(),
    ]


def project_kernel(
    tok_in, wq_in, wk_in, wv_in, down_ref, up_ref, cos_ref, sin_ref, out_ref,
    tok, weights, acc, low, send_sem, recv_sem, local_sem,
):
    me = Place()
    w_in = (wq_in, wk_in, wv_in)
    own_cols = pl.multiple_of(me.xl * 256, 256)
    other_cols = pl.multiple_of((1 - me.xl) * 256, 256)
    local = [pltpu.make_async_copy(tok_in, tok.at[me.h, me.xl], local_sem.at[0])]
    for j in range(3):
        local.append(
            pltpu.make_async_copy(
                w_in[j].at[:, pl.ds(own_cols, 256)], weights.at[j, me.z, me.xl, me.k], local_sem.at[1 + j]
            )
        )
    for copy in local:
        copy.start()
    greet(all_neighbours(me))
    sends = Sends(send_sem, recv_sem)
    trade = []
    for j in range(3):
        trade.append(
            sends.start(
                w_in[j].at[:, pl.ds(other_cols, 256)],
                weights.at[j, me.z, me.xl, me.k],
                me.partner(),
                sends.slot(),
            )
        )
    for copy in local[1:]:
        copy.wait()
    own_ring = RingZ(sends, me, lambda z, k: weights.at[:, z, me.xl, k])
    other_ring = RingZ(sends, me, lambda z, k: weights.at[:, z, 1 - me.xl, k])
    own_ring.start()
    local[0].wait()

    def block(half, x, y):
        return tok.at[lax.div(x, 2) * 4 + y, lax.rem(x, 2), pl.ds(half * 128, 128)]

    events = PlaneGather(sends, me, block).events()
    events[0]()
    events[1]()
    for copy in trade:
        copy.wait_recv()
    other_ring.start()
    own_ring.take_ahead(1)
    own_ring.take_back(1)
    events[2]()
    events[3]()
    events[4]()
    other_ring.take_ahead(1)
    other_ring.take_back(1)
    events[5]()
    events[6]()
    own_ring.take_ahead(2)
    own_ring.take_back(2)
    events[7]()
    other_ring.take_ahead(2)
    other_ring.take_back(2)
    events[8]()

    def multiply(step, first=False):
        chunk = lax.rem(me.z + 8 + step, 8)
        left = tok[chunk].reshape(512, 512)
        for j in range(3):
            part = jnp.dot(left, weights[j, chunk].reshape(512, 256), preferred_element_type=F32)
            if first:
                acc[j] = part
            else:
                acc[j] += part

    def low_rank(chunk, total):
        left = tok[chunk].reshape(512, 512)
        cols = pl.multiple_of(chunk * 512, 512)
        return total + lax.dot_general(
            left, down_ref[:, pl.ds(cols, 512)], (((1,), (1,)), ((), ())), preferred_element_type=F32
        )

    def shared(key):
        own_ring.wait_shared(key)
        other_ring.wait_shared(key)

    shared("own")
    multiply(0, True)
    low[...] = lax.fori_loop(0, 4, low_rank, jnp.zeros((512, 24), F32))
    own_ring.take_ahead(3)
    own_ring.take_back(3)
    for s in (1, 2):
        shared(("a", s))
        shared(("b", s))
        multiply(s)
        multiply(-s)
    other_ring.take_ahead(3)
    other_ring.take_back(3)
    own_ring.take_ahead(4)
    low[...] = lax.fori_loop(4, 8, low_rank, low[...])
    shared(("a", 3))
    shared(("b", 3))
    multiply(3)
    multiply(-3)
    other_ring.take_ahead(4)
    shared(("a", 4))
    multiply(4)
    rank = low[...].astype(BF16)
    rank_of = lax.broadcasted_iota(jnp.int32, (512, 24), 1) // 8
    for j in range(3):
        mine = jnp.where(rank_of == j, rank, jnp.zeros_like(rank))
        full = acc[j] + 2.0 * jnp.dot(mine, up_ref[:, pl.ds(own_cols, 256)], preferred_element_type=F32)
        for head in range(2):
            part = full[:, head * HEAD : (head + 1) * HEAD]
            if j < 2:
                part = part * cos_ref[...] + pltpu.roll(part, HEAD // 2, 1) * sin_ref[...]
            out_ref[head, j] = part.astype(BF16)
    sends.finish()


def project(tokens, wq, wk, wv, down, up, cosine, sine):
    slots = 64
    any_spec = pl.BlockSpec(memory_space=pl.ANY)
    vmem = pl.BlockSpec(memory_space=pltpu.VMEM)
    return pl.pallas_call(
        project_kernel,
        out_shape=jax.ShapeDtypeStruct((2, 3, 2 * TOK, HEAD), BF16),
        in_specs=[any_spec] * 4 + [vmem] * 4,
        out_specs=vmem,
        scratch_shapes=[
            pltpu.VMEM((8, 2, TOK, 512), BF16),
            pltpu.VMEM((3, 8, 2, 2, 128, 256), BF16),
            pltpu.VMEM((3, 512, 256), F32),
            pltpu.VMEM((512, 24), F32),
            pltpu.SemaphoreType.DMA((slots + 1,)),
            pltpu.SemaphoreType.DMA((slots + 1,)),
            pltpu.SemaphoreType.DMA((4,)),
        ],
        compiler_params=pltpu.CompilerParams(
            collective_id=0, has_side_effects=True, vmem_limit_bytes=40 << 20
        ),
        name="project",
    )(tokens, wq, wk, wv, down, up, cosine, sine)


def attend_kernel(qkv_in, out_ref, query, kv, total, top, denom, far_out, send_sem, recv_sem, local_sem):
    me = Place()
    p = lax.rem(me.z + 8 - 2 * me.xh, 4)
    mine = lax.div(p, 2)
    own_slot = mine
    lower = p + mine * (3 - 2 * p)

    def plane(q):
        return me.at(z=lax.rem(me.z + 8 - p + q, 8))

    def receive_q():
        return pltpu.make_async_remote_copy(
            qkv_in.at[0, 0], query.at[1 - own_slot], send_sem.at[0], recv_sem.at[0],
            device_id=me.sibling(), device_id_type=MESH,
        )

    local = [
        pltpu.make_async_copy(qkv_in.at[mine, 0], query.at[own_slot], local_sem.at[0]),
        pltpu.make_async_copy(qkv_in.at[mine, pl.ds(1, 2)], kv.at[p, me.k], local_sem.at[1]),
    ]
    for copy in local:
        copy.start()
    greet([plane(lax.rem(p + 1, 4)), plane(lax.rem(p + 2, 4)), plane(lax.rem(p + 3, 4)), me.sibling()])

    def kv_copy(src, b, device, send):
        return pltpu.make_async_remote_copy(
            src, kv.at[b, me.k], send_sem.at[send], recv_sem.at[1 + b],
            device_id=device, device_id_type=MESH,
        )

    def q_copy(head, slot, device):
        return pltpu.make_async_remote_copy(
            qkv_in.at[head, 0], query.at[slot], send_sem.at[0], recv_sem.at[0],
            device_id=device, device_id_type=MESH,
        )

    def kv_in(head):
        return qkv_in.at[head, pl.ds(1, 2)]

    def share(b, src):
        return pltpu.make_async_remote_copy(
            src, kv.at[b, me.k], send_sem.at[5 + b], recv_sem.at[5 + b],
            device_id=me.sibling(), device_id_type=MESH,
        )

    @pl.when(p == 0)
    def _():
        kv_copy(kv_in(0), 0, plane(1), 1).start()
        kv_copy(kv_in(1), 0, plane(2), 2).start()
        q_copy(1, 0, plane(3)).start()

    @pl.when(p == 1)
    def _():
        kv_copy(kv_in(1), 1, plane(2), 2).start()
        q_copy(1, 0, plane(2)).start()
        kv_copy(kv_in(0), 1, plane(0), 1).start()

    @pl.when(p == 2)
    def _():
        kv_copy(kv_in(0), 2, plane(1), 1).start()
        q_copy(0, 1, plane(1)).start()
        kv_copy(kv_in(1), 2, plane(3), 2).start()

    @pl.when(p == 3)
    def _():
        q_copy(0, 1, plane(0)).start()
        kv_copy(kv_in(0), 3, plane(0), 1).start()

    share(p, kv_in(mine)).start()
    top[...] = jnp.full_like(top, -1e30)
    denom[...] = jnp.zeros_like(denom)
    total[...] = jnp.zeros_like(total)
    for copy in local:
        copy.wait()

    rows = lax.broadcasted_iota(jnp.int32, (TOK, 512), 0)
    cols = lax.broadcasted_iota(jnp.int32, (TOK, 512), 1)
    key_place = lax.div(cols, 256) * 512 + lax.rem(cols, 256)
    scale = HEAD ** (-0.5)

    def update(slot, b, half, core, masked):
        q = query[slot, pl.ds(half * TOK, TOK)]
        scores = lax.dot_general(
            q, kv[b, core, 0], (((1,), (1,)), ((), ())), preferred_element_type=F32
        ) * scale
        if masked:
            allowed = key_place + core * 256 <= rows + half * 512 + me.k * 256
            scores = jnp.where(allowed, scores, -1e30)
        part = pl.ds(half * TOK, TOK)
        old = top[slot, part]
        new = jnp.maximum(old, jnp.max(scores, axis=1, keepdims=True))
        weights = jnp.exp(scores - new)
        if masked:
            weights = jnp.where(allowed, weights, 0.0)
        factor = jnp.exp(old - new)
        top[slot, part] = new
        denom[slot, part] = denom[slot, part] * factor + jnp.sum(weights, axis=1, keepdims=True)
        total[slot, part] = total[slot, part] * factor + jnp.dot(
            weights.astype(BF16), kv[b, core, 1], preferred_element_type=F32
        )

    def block_of(slot):
        return lower + slot * (3 - 2 * lower)

    def pair(slot, b):
        @pl.when(block_of(slot) > b)
        def _():
            for half in range(2):
                for core in range(2):
                    update(slot, b, half, core, False)

        @pl.when(block_of(slot) == b)
        def _():
            for half in range(2):
                for core in range(2):
                    update(slot, b, half, core, True)

    def step(t, carry):
        b = jnp.where(
            p == 0, t, jnp.where(p == 3, 3 - t, jnp.where(p == 1, lax.rem(t + 1, 3), 2 - t))
        )
        used = (p == 0) | (p == 3) | (t < 3)

        @pl.when(used & (t > 0))
        def _():
            kv_copy(kv.at[b, me.k], b, me.sibling(), 1).wait_recv()
            share(b, kv.at[b, me.k]).start()

            @pl.when((p == 1) & (b == 2))
            def _():
                kv_copy(kv.at[2, me.k], 2, plane(0), 3).start()

            @pl.when(p == 2)
            def _():
                kv_copy(kv.at[b, me.k], b, plane(3), 3 + lax.rem(b, 2)).start()

        @pl.when(t == 1)
        def _():
            receive_q().wait_recv()

        @pl.when(used)
        def _():
            share(b, kv.at[b, me.k]).wait_recv()
            own_first = jnp.where(t == 0, own_slot, 0)
            count = jnp.where(t == 0, 1, 2)

            def slots(i, c):
                pair(own_first + i, b)
                return c

            lax.fori_loop(0, count, slots, 0)

            @pl.when((t == 1) & (block_of(1 - own_slot) >= p))
            def _():
                pair(1 - own_slot, p)

        return carry

    lax.fori_loop(0, 4, step, 0)
    for slot in range(2):
        result = (total[slot] / denom[slot]).astype(BF16)
        far_out[slot] = result
    give = pltpu.make_async_remote_copy(
        far_out.at[1 - own_slot], out_ref.at[mine], send_sem.at[9], recv_sem.at[9],
        device_id=plane(3 - p), device_id_type=MESH,
    )
    give.start()
    out_ref[mine] = far_out[own_slot]
    q_copy(0, 0, me.sibling()).wait_send()
    kv_copy(kv_in(0), 0, me.sibling(), 1).wait_send()

    @pl.when(p < 3)
    def _():
        kv_copy(kv_in(0), 0, me.sibling(), 2).wait_send()

    @pl.when(p == 1)
    def _():
        kv_copy(kv_in(0), 0, me.sibling(), 3).wait_send()

    @pl.when(p == 2)
    def _():
        kv_copy(kv_in(0), 0, me.sibling(), 3).wait_send()
        kv_copy(kv_in(0), 0, me.sibling(), 4).wait_send()

    for b in range(3):
        share(b, kv_in(0)).wait_send()

    @pl.when((p == 0) | (p == 3))
    def _():
        share(3, kv_in(0)).wait_send()

    give.wait()


def attend(qkv):
    vmem = pl.BlockSpec(memory_space=pltpu.VMEM)
    return pl.pallas_call(
        attend_kernel,
        out_shape=jax.ShapeDtypeStruct((2, 2 * TOK, HEAD), BF16),
        in_specs=[pl.BlockSpec(memory_space=pl.ANY)],
        out_specs=vmem,
        scratch_shapes=[
            pltpu.VMEM((2, 512, HEAD), BF16),
            pltpu.VMEM((4, 2, 2, 512, HEAD), BF16),
            pltpu.VMEM((2, 512, HEAD), F32),
            pltpu.VMEM((2, 512, 1), F32),
            pltpu.VMEM((2, 512, 1), F32),
            pltpu.VMEM((2, 512, HEAD), BF16),
            pltpu.SemaphoreType.DMA((10,)),
            pltpu.SemaphoreType.DMA((10,)),
            pltpu.SemaphoreType.DMA((2,)),
        ],
        compiler_params=pltpu.CompilerParams(
            collective_id=1, has_side_effects=True, vmem_limit_bytes=40 << 20
        ),
        name="attend",
    )(qkv)


def merge_kernel(
    heads_in, wo_in, out_ref, merged, weights, acc, stage, send_sem, recv_sem, local_sem
):
    me = Place()
    own_cols = pl.multiple_of(me.xl * 256, 256)
    other_cols = pl.multiple_of((1 - me.xl) * 256, 256)
    local = [
        pltpu.make_async_copy(heads_in, merged.at[me.h, me.xl], local_sem.at[0]),
        pltpu.make_async_copy(
            wo_in.at[:, pl.ds(own_cols, 256)], weights.at[me.z, me.xl, me.k], local_sem.at[1]
        ),
    ]
    for copy in local:
        copy.start()
    greet(all_neighbours(me))
    sends = Sends(send_sem, recv_sem)
    trade = sends.start(
        wo_in.at[:, pl.ds(other_cols, 256)],
        weights.at[me.z, me.xl, me.k],
        me.partner(),
        sends.slot(),
    )
    for copy in local:
        copy.wait()

    def block(half, x, y):
        return merged.at[lax.div(x, 2) * 4 + y, lax.rem(x, 2), half]

    events = PlaneGather(sends, me, block).events()
    ring = RingZ(sends, me, lambda z, k: weights.at[z, :, k])
    events[0]()
    trade.wait_recv()
    ring.start()
    events[1]()
    events[2]()
    ring.take_ahead(1)
    ring.take_back(1)
    events[3]()
    events[4]()
    ring.take_ahead(2)
    ring.take_back(2)
    events[5]()
    ring.take_ahead(3)
    ring.take_back(3)
    events[6]()
    ring.take_ahead(4)
    events[7]()
    ring.wait_shared("own")
    for s in (1, 2, 3):
        ring.wait_shared(("a", s))
        ring.wait_shared(("b", s))
    ring.wait_shared(("a", 4))
    events[8]()

    def multiply(h, total):
        for xl in range(2):
            left = jnp.concatenate([merged[h, xl, 0], merged[h, xl, 1]], axis=1)
            total = total + jnp.dot(
                left, weights[h, xl].reshape(256, 256), preferred_element_type=F32
            )
        return total

    acc[...] = jnp.zeros_like(acc)

    @pl.loop(0, 8)
    def _(h):
        acc[...] = multiply(h, acc[...])

    stage[0] = acc[pl.ds(0, TOK)].astype(BF16)
    stage[1] = acc[pl.ds(TOK, TOK)].astype(BF16)
    give = sends.start(
        stage.at[1 - me.xl], out_ref.at[:, pl.ds(own_cols, 256)], me.partner(), sends.slot()
    )
    out_ref[:, pl.ds(own_cols, 256)] = stage[me.xl]
    give.wait_recv()
    sends.finish()


def merge(heads, wo):
    any_spec = pl.BlockSpec(memory_space=pl.ANY)
    vmem = pl.BlockSpec(memory_space=pltpu.VMEM)
    return pl.pallas_call(
        merge_kernel,
        out_shape=jax.ShapeDtypeStruct((TOK, 512), BF16),
        in_specs=[any_spec] * 2,
        out_specs=vmem,
        scratch_shapes=[
            pltpu.VMEM((8, 2, 2, 512, HEAD), BF16),
            pltpu.VMEM((8, 2, 2, 128, 256), BF16),
            pltpu.VMEM((512, 256), F32),
            pltpu.VMEM((2, TOK, 256), BF16),
            pltpu.SemaphoreType.DMA((64,)),
            pltpu.SemaphoreType.DMA((64,)),
            pltpu.SemaphoreType.DMA((2,)),
        ],
        compiler_params=pltpu.CompilerParams(
            collective_id=2, has_side_effects=True, vmem_limit_bytes=40 << 20
        ),
        name="merge",
    )(heads, wo)


def rotary_tables():
    c = lax.axis_index("ctx")
    base = lax.div(c, 4) * 1024 + lax.rem(c, 2) * 256
    rows = jnp.arange(512, dtype=jnp.int32)
    positions = base + (rows // 256) * 512 + rows % 256
    inverse_freq = 10000.0 ** (-(jnp.arange(HEAD // 2, dtype=F32) * 2.0) / HEAD)
    angles = positions.astype(F32)[:, None] * inverse_freq[None, :]
    cosine, sine = jnp.cos(angles), jnp.sin(angles)
    return jnp.concatenate([cosine, cosine], 1), jnp.concatenate([-sine, sine], 1)


def per_device(tokens, wq, wk, wv, wo, down, up):
    cosine, sine = rotary_tables()
    qkv = project(tokens, wq, wk, wv, down.reshape(24, D), up.reshape(24, 512), cosine, sine)
    heads = attend(qkv)
    return merge(heads, wo)


def solution(mesh):
    placed = P("ctx", "head")
    return jax.shard_map(
        per_device,
        mesh=mesh,
        in_specs=(placed,) * 5 + (P(), P(None, None, "head")),
        out_specs=placed,
        check_vma=False,
    )
```

time: 374 us -> 132 us (0.35)
  the two profiles are of different devices: /device:TPU:24 before, /device:TPU:2 now
where the time goes in v1:
time: 132 us
  Pallas kernels  129 us (98%)
  local copies, waits for them, and re-layouts  1.65 us (1%)
    pallas_call x1, Pallas kernels, project(): pl.pallas_call(project_kernel, out_shape=jax.ShapeDtypeStruct((2, 3, 2 *...  45.3 us
    pallas_call x1, Pallas kernels, attend(): pl.pallas_call(attend_kernel, out_shape=jax.ShapeDtypeStruct((2, 2 * TOK,...  42.6 us
    pallas_call x1, Pallas kernels, merge(): pl.pallas_call(merge_kernel, out_shape=jax.ShapeDtypeStruct((TOK, 512), B...  40.9 us

profile of v1, /device:TPU:2, one launch (start us, length us, event | category | flops | bytes accessed | tf_op | source)
XLA Modules:
  0.0 131.7 jit_solution(10109052456333739483)
XLA Ops:
  0.0 1.0 fusion
  1.0 0.0 copy-start
  1.0 0.0 copy-start.1
  1.0 0.0 copy-start.2
  1.1 0.0 copy-start.3
  1.1 0.0 copy-start.4
  1.1 0.0 copy-start.6
  1.1 0.2 pad_maximum_fusion
  1.3 0.7 copy-done
  2.0 0.1 copy-done.1
  2.0 0.1 copy-done.2
  2.1 0.1 copy-done.3
  2.2 0.0 copy-done.4
  2.2 0.0 copy-done.6
  2.2 45.3 %project.1.qkv_in = bf16[2,3,512,128]{3,2,1,0:T(8,128)(2,1)S(1)} custom-call(bf16[256,512]{1,0:T(8,128)(2,1)S(1)} %copy-done, bf16[128,512]{1,0:T(8,128)(2,1)S(1)} %copy-done.2, bf16[128,512]{1,0:T(8,128)(2,1)S(1)} %copy-done.3, bf16[128,512]{1,0:T(8,128)(2,1)S(1)} %copy-done.4, bf16[24,4096]{1,0:T(8,128)(2,1)S(1)} %bitcast.2, bf16[24,512]{1,0:T(8,128)(2,1)S(1)} %bitcast.3, ...), custom_call_target="tpu_custom_call" | custom-call | tf_op jit(solution)/shard_map/project/pallas_call | solution.py:335
  47.5 0.0 copy-start.5
  47.5 42.6 %attend.1.heads_in = bf16[2,512,128]{2,1,0:T(8,128)(2,1)S(1)} custom-call(bf16[2,3,512,128]{3,2,1,0:T(8,128)(2,1)S(1)} %project.1.qkv_in), custom_call_target="tpu_custom_call" | custom-call | tf_op jit(solution)/shard_map/attend/pallas_call | solution.py:552
  90.1 0.0 copy-done.5
  90.1 40.9 %merge.1 = bf16[256,512]{1,0:T(8,128)(2,1)S(1)} custom-call(bf16[2,512,128]{2,1,0:T(8,128)(2,1)S(1)} %attend.1.heads_in, bf16[128,512]{1,0:T(8,128)(2,1)S(1)} %copy-done.5), custom_call_target="tpu_custom_call" | custom-call | tf_op jit(solution)/shard_map/merge/pallas_call | solution.py:656
  131.0 0.7 copy.9
  (2 shorter events, 0.0 us)
Async XLA Ops:
  1.0 1.0 copy-start
  1.0 1.0 copy-start.1
  1.0 1.1 copy-start.2
  1.1 1.1 copy-start.3
  1.1 1.1 copy-start.4
  1.1 1.1 copy-start.6
  47.5 42.6 %copy-start.5 = (bf16[128,512]{1,0:T(8,128)(2,1)S(1)}, bf16[128,512]{1,0:T(8,128)(2,1)}, u32[]{:S(2)}) copy-start(bf16[128,512]{1,0:T(8,128)(2,1)} %wo_in.1) | copy-start | bytes 393220

commit v2 on v1

--- a/solution.py
+++ b/solution.py
@@ -162,6 +162,51 @@
         return [start, ahead, back, second(0), far, second(1), second(2), second(3), finish]
 
 
+class HeadGather:
+    def __init__(self, sends, me, block):
+        self.me, self.sends, self.block = me, sends, block
+        far = 1 - me.xh
+        self.own_a = Ring4(sends, me.y, me.sigma, me.to_y, lambda a: block(0, me.xh, a))
+        self.far_a = Ring4(sends, me.y, me.sigma, me.to_y, lambda a: block(0, far, a))
+        self.own_b = Ring4(sends, me.y, me.sigma, me.to_y, lambda a: block(1, me.xh, a))
+        self.crossed = []
+
+    def cross(self, half, step):
+        block = self.block(half, self.me.xh, lax.rem(self.me.y + 4 + step * self.me.sigma, 4))
+        self.crossed.append(
+            self.sends.start(block, block, self.me.to_x(2), self.sends.slot())
+        )
+
+    def start(self):
+        self.cross(0, 0)
+        self.own_b.start()
+        self.cross(1, 0)
+        self.own_a.start()
+
+    def step_1(self):
+        self.own_b.forward()
+        self.cross(1, -1)
+        self.own_b.wait_back()
+        self.cross(1, 1)
+
+    def step_2(self):
+        self.crossed[0].wait_recv()
+        self.far_a.start()
+        self.own_a.forward()
+
+    def step_3(self):
+        self.own_b.wait_far()
+        self.cross(1, -2)
+        self.far_a.forward()
+
+    def finish(self):
+        for ring in (self.own_a, self.far_a):
+            ring.wait_back()
+            ring.wait_far()
+        for copy in self.crossed[1:]:
+            copy.wait_recv()
+
+
 class RingZ:
     def __init__(self, sends, me, block):
         self.sends, self.me, self.block = sends, me, block
@@ -200,26 +245,23 @@
         self.shared[key].wait_recv()
 
 
-def all_neighbours(me):
-    return [
-        me.to_z(1),
-        me.to_z(-1),
-        me.to_x(1),
-        me.to_x(-1),
-        me.to_y(1),
-        me.to_y(-1),
-        me.sibling(),
-    ]
-
-
-def project_kernel(
-    tok_in, wq_in, wk_in, wv_in, down_ref, up_ref, cos_ref, sin_ref, out_ref,
-    tok, weights, acc, low, send_sem, recv_sem, local_sem,
+def layer_kernel(
+    tok_in, wq_in, wk_in, wv_in, wo_in, down_ref, up_ref, cos_ref, sin_ref, out_ref,
+    tok, weights, acc, low, qkv, query, kv, total, top, denom, heads_out, merged, wo,
+    send_sem, recv_sem, pair_send, pair_recv, local_sem,
 ):
     me = Place()
     w_in = (wq_in, wk_in, wv_in)
     own_cols = pl.multiple_of(me.xl * 256, 256)
     other_cols = pl.multiple_of((1 - me.xl) * 256, 256)
+    p = lax.rem(me.z + 8 - 2 * me.xh, 4)
+    mine = lax.div(p, 2)
+    lower = p + mine * (3 - 2 * p)
+
+    def plane(q, x=None):
+        return me.at(z=lax.rem(me.z + 8 - p + q, 8), x=x)
+
+    partner_x = me.xh * 2 + 1 - me.xl
     local = [pltpu.make_async_copy(tok_in, tok.at[me.h, me.xl], local_sem.at[0])]
     for j in range(3):
         local.append(
@@ -227,9 +269,15 @@
                 w_in[j].at[:, pl.ds(own_cols, 256)], weights.at[j, me.z, me.xl, me.k], local_sem.at[1 + j]
             )
         )
+    local.append(pltpu.make_async_copy(wo_in, wo.at[me.z, me.xl, me.k], local_sem.at[4]))
     for copy in local:
         copy.start()
-    greet(all_neighbours(me))
+    greet(
+        [
+            me.to_z(1), me.to_z(-1), me.to_x(1), me.to_x(-1), me.to_x(2), me.to_y(1), me.to_y(-1), me.sibling(),
+            plane(lax.rem(p + 1, 4)), plane(lax.rem(p + 2, 4)), plane(lax.rem(p + 3, 4)), plane(3 - p, partner_x),
+        ]
+    )
     sends = Sends(send_sem, recv_sem)
     trade = []
     for j in range(3):
@@ -272,21 +320,24 @@
     other_ring.take_ahead(2)
     other_ring.take_back(2)
     events[8]()
+    trade_wo = sends.start(
+        wo.at[me.z, me.xl, me.k], wo.at[me.z, me.xl, me.k], me.partner(), sends.slot()
+    )
 
     def multiply(step, first=False):
         chunk = lax.rem(me.z + 8 + step, 8)
         left = tok[chunk].reshape(512, 512)
-        for j in range(3):
+        for j in (1, 2, 0):
             part = jnp.dot(left, weights[j, chunk].reshape(512, 256), preferred_element_type=F32)
             if first:
                 acc[j] = part
             else:
                 acc[j] += part
 
-    def low_rank(chunk, total):
+    def low_rank(chunk, so_far):
         left = tok[chunk].reshape(512, 512)
         cols = pl.multiple_of(chunk * 512, 512)
-        return total + lax.dot_general(
+        return so_far + lax.dot_general(
             left, down_ref[:, pl.ds(cols, 512)], (((1,), (1,)), ((), ())), preferred_element_type=F32
         )
 
@@ -312,122 +363,87 @@
     shared(("b", 3))
     multiply(3)
     multiply(-3)
+    top[...] = jnp.full_like(top, -1e30)
+    denom[...] = jnp.zeros_like(denom)
+    total[...] = jnp.zeros_like(total)
     other_ring.take_ahead(4)
     shared(("a", 4))
     multiply(4)
     rank = low[...].astype(BF16)
     rank_of = lax.broadcasted_iota(jnp.int32, (512, 24), 1) // 8
-    for j in range(3):
-        mine = jnp.where(rank_of == j, rank, jnp.zeros_like(rank))
-        full = acc[j] + 2.0 * jnp.dot(mine, up_ref[:, pl.ds(own_cols, 256)], preferred_element_type=F32)
+
+    def finish_projection(j):
+        part_rank = jnp.where(rank_of == j, rank, jnp.zeros_like(rank))
+        full = acc[j] + 2.0 * jnp.dot(
+            part_rank, up_ref[:, pl.ds(own_cols, 256)], preferred_element_type=F32
+        )
         for head in range(2):
             part = full[:, head * HEAD : (head + 1) * HEAD]
             if j < 2:
                 part = part * cos_ref[...] + pltpu.roll(part, HEAD // 2, 1) * sin_ref[...]
-            out_ref[head, j] = part.astype(BF16)
-    sends.finish()
-
-
-def project(tokens, wq, wk, wv, down, up, cosine, sine):
-    slots = 64
-    any_spec = pl.BlockSpec(memory_space=pl.ANY)
-    vmem = pl.BlockSpec(memory_space=pltpu.VMEM)
-    return pl.pallas_call(
-        project_kernel,
-        out_shape=jax.ShapeDtypeStruct((2, 3, 2 * TOK, HEAD), BF16),
-        in_specs=[any_spec] * 4 + [vmem] * 4,
-        out_specs=vmem,
-        scratch_shapes=[
-            pltpu.VMEM((8, 2, TOK, 512), BF16),
-            pltpu.VMEM((3, 8, 2, 2, 128, 256), BF16),
-            pltpu.VMEM((3, 512, 256), F32),
-            pltpu.VMEM((512, 24), F32),
-            pltpu.SemaphoreType.DMA((slots + 1,)),
-            pltpu.SemaphoreType.DMA((slots + 1,)),
-            pltpu.SemaphoreType.DMA((4,)),
-        ],
-        compiler_params=pltpu.CompilerParams(
-            collective_id=0, has_side_effects=True, vmem_limit_bytes=40 << 20
-        ),
-        name="project",
-    )(tokens, wq, wk, wv, down, up, cosine, sine)
-
-
-def attend_kernel(qkv_in, out_ref, query, kv, total, top, denom, far_out, send_sem, recv_sem, local_sem):
-    me = Place()
-    p = lax.rem(me.z + 8 - 2 * me.xh, 4)
-    mine = lax.div(p, 2)
-    own_slot = mine
-    lower = p + mine * (3 - 2 * p)
-
-    def plane(q):
-        return me.at(z=lax.rem(me.z + 8 - p + q, 8))
-
-    def receive_q():
-        return pltpu.make_async_remote_copy(
-            qkv_in.at[0, 0], query.at[1 - own_slot], send_sem.at[0], recv_sem.at[0],
-            device_id=me.sibling(), device_id_type=MESH,
-        )
-
-    local = [
-        pltpu.make_async_copy(qkv_in.at[mine, 0], query.at[own_slot], local_sem.at[0]),
-        pltpu.make_async_copy(qkv_in.at[mine, pl.ds(1, 2)], kv.at[p, me.k], local_sem.at[1]),
-    ]
-    for copy in local:
-        copy.start()
-    greet([plane(lax.rem(p + 1, 4)), plane(lax.rem(p + 2, 4)), plane(lax.rem(p + 3, 4)), me.sibling()])
+            qkv[head, j] = part.astype(BF16)
 
     def kv_copy(src, b, device, send):
         return pltpu.make_async_remote_copy(
-            src, kv.at[b, me.k], send_sem.at[send], recv_sem.at[1 + b],
+            src, kv.at[b, me.k], pair_send.at[send], pair_recv.at[1 + b],
             device_id=device, device_id_type=MESH,
         )
 
     def q_copy(head, slot, device):
         return pltpu.make_async_remote_copy(
-            qkv_in.at[head, 0], query.at[slot], send_sem.at[0], recv_sem.at[0],
+            qkv.at[head, 0], query.at[slot], pair_send.at[0], pair_recv.at[0],
             device_id=device, device_id_type=MESH,
         )
 
-    def kv_in(head):
-        return qkv_in.at[head, pl.ds(1, 2)]
+    def kv_of(head):
+        return qkv.at[head, pl.ds(1, 2)]
 
     def share(b, src):
         return pltpu.make_async_remote_copy(
-            src, kv.at[b, me.k], send_sem.at[5 + b], recv_sem.at[5 + b],
+            src, kv.at[b, me.k], pair_send.at[5 + b], pair_recv.at[5 + b],
             device_id=me.sibling(), device_id_type=MESH,
         )
 
+    finish_projection(1)
+    finish_projection(2)
+
     @pl.when(p == 0)
     def _():
-        kv_copy(kv_in(0), 0, plane(1), 1).start()
-        kv_copy(kv_in(1), 0, plane(2), 2).start()
+        kv_copy(kv_of(0), 0, plane(1), 1).start()
+        kv_copy(kv_of(1), 0, plane(2), 2).start()
+
+    @pl.when(p == 1)
+    def _():
+        kv_copy(kv_of(1), 1, plane(2), 2).start()
+
+    @pl.when(p == 2)
+    def _():
+        kv_copy(kv_of(0), 2, plane(1), 1).start()
+
+    share(p, kv_of(mine)).start()
+    finish_projection(0)
+
+    @pl.when(p == 0)
+    def _():
         q_copy(1, 0, plane(3)).start()
 
     @pl.when(p == 1)
     def _():
-        kv_copy(kv_in(1), 1, plane(2), 2).start()
         q_copy(1, 0, plane(2)).start()
-        kv_copy(kv_in(0), 1, plane(0), 1).start()
+        kv_copy(kv_of(0), 1, plane(0), 1).start()
 
     @pl.when(p == 2)
     def _():
-        kv_copy(kv_in(0), 2, plane(1), 1).start()
         q_copy(0, 1, plane(1)).start()
-        kv_copy(kv_in(1), 2, plane(3), 2).start()
+        kv_copy(kv_of(1), 2, plane(3), 2).start()
 
     @pl.when(p == 3)
     def _():
         q_copy(0, 1, plane(0)).start()
-        kv_copy(kv_in(0), 3, plane(0), 1).start()
-
-    share(p, kv_in(mine)).start()
-    top[...] = jnp.full_like(top, -1e30)
-    denom[...] = jnp.zeros_like(denom)
-    total[...] = jnp.zeros_like(total)
-    for copy in local:
-        copy.wait()
-
+        kv_copy(kv_of(0), 3, plane(0), 1).start()
+
+    query[mine] = qkv[mine, 0]
+    kv[p, me.k] = qkv[mine, 1:3]
     rows = lax.broadcasted_iota(jnp.int32, (TOK, 512), 0)
     cols = lax.broadcasted_iota(jnp.int32, (TOK, 512), 1)
     key_place = lax.div(cols, 256) * 512 + lax.rem(cols, 256)
@@ -444,14 +460,14 @@
         part = pl.ds(half * TOK, TOK)
         old = top[slot, part]
         new = jnp.maximum(old, jnp.max(scores, axis=1, keepdims=True))
-        weights = jnp.exp(scores - new)
+        probs = jnp.exp(scores - new)
         if masked:
-            weights = jnp.where(allowed, weights, 0.0)
+            probs = jnp.where(allowed, probs, 0.0)
         factor = jnp.exp(old - new)
         top[slot, part] = new
-        denom[slot, part] = denom[slot, part] * factor + jnp.sum(weights, axis=1, keepdims=True)
+        denom[slot, part] = denom[slot, part] * factor + jnp.sum(probs, axis=1, keepdims=True)
         total[slot, part] = total[slot, part] * factor + jnp.dot(
-            weights.astype(BF16), kv[b, core, 1], preferred_element_type=F32
+            probs.astype(BF16), kv[b, core, 1], preferred_element_type=F32
         )
 
     def block_of(slot):
@@ -491,187 +507,153 @@
 
         @pl.when(t == 1)
         def _():
-            receive_q().wait_recv()
+            q_copy(0, 1 - mine, me.sibling()).wait_recv()
 
         @pl.when(used)
         def _():
             share(b, kv.at[b, me.k]).wait_recv()
-            own_first = jnp.where(t == 0, own_slot, 0)
+            first = jnp.where(t == 0, mine, 0)
             count = jnp.where(t == 0, 1, 2)
 
             def slots(i, c):
-                pair(own_first + i, b)
+                pair(first + i, b)
                 return c
 
             lax.fori_loop(0, count, slots, 0)
 
-            @pl.when((t == 1) & (block_of(1 - own_slot) >= p))
+            @pl.when((t == 1) & (block_of(1 - mine) >= p))
             def _():
-                pair(1 - own_slot, p)
+                pair(1 - mine, p)
 
         return carry
 
     lax.fori_loop(0, 4, step, 0)
-    for slot in range(2):
-        result = (total[slot] / denom[slot]).astype(BF16)
-        far_out[slot] = result
-    give = pltpu.make_async_remote_copy(
-        far_out.at[1 - own_slot], out_ref.at[mine], send_sem.at[9], recv_sem.at[9],
-        device_id=plane(3 - p), device_id_type=MESH,
-    )
-    give.start()
-    out_ref[mine] = far_out[own_slot]
+    trade_wo.wait_recv()
+    ring_a = RingZ(sends, me, lambda z, k: wo.at[z, me.xl, k])
+    ring_b = RingZ(sends, me, lambda z, k: wo.at[z, 1 - me.xl, k])
+    give = []
+    place = merged.at[me.h, me.xl * 2 + mine]
+
+    far_slot = 1 - mine
+    heads_out[far_slot] = (total[far_slot] / denom[far_slot]).astype(BF16)
+    for x, r in ((me.x, me.xl), (partner_x, 1 - me.xl)):
+        rows_r = pl.ds(pl.multiple_of(r * TOK, TOK), TOK)
+        give.append(sends.start(heads_out.at[far_slot, rows_r], place, plane(3 - p, x), sends.slot()))
+    heads_out[mine] = (total[mine] / denom[mine]).astype(BF16)
+    rows_r = pl.ds(pl.multiple_of((1 - me.xl) * TOK, TOK), TOK)
+    give.append(sends.start(heads_out.at[mine, rows_r], place, me.partner(), sends.slot()))
+    merged[me.h, me.xl * 2 + mine] = heads_out[mine, pl.ds(pl.multiple_of(me.xl * TOK, TOK), TOK)]
+    ring_a.start()
+    ring_b.start()
+
+    for copy in give:
+        copy.wait_recv()
+    gather = HeadGather(sends, me, lambda half, xh, y: merged.at[xh * 4 + y, pl.ds(half * 2, 2)])
+    gather.start()
+    ring_a.take_ahead(1)
+    ring_a.take_back(1)
+    gather.step_1()
+    ring_b.take_ahead(1)
+    ring_b.take_back(1)
+    gather.step_2()
+    ring_a.take_ahead(2)
+    ring_a.take_back(2)
+    gather.step_3()
+    ring_b.take_ahead(2)
+    ring_b.take_back(2)
+    ring_a.take_ahead(3)
+    ring_a.take_back(3)
+    ring_b.take_ahead(3)
+    ring_b.take_back(3)
+    gather.finish()
+
+    def merge(step, so_far):
+        h = lax.rem(me.z + 8 + step, 8)
+        for half in range(2):
+            left = jnp.concatenate([merged[h, 2 * half], merged[h, 2 * half + 1]], axis=1)
+            so_far = so_far + jnp.dot(
+                left, wo[h, half].reshape(256, 512), preferred_element_type=F32
+            )
+        return so_far
+
+    def ready(key):
+        ring_a.wait_shared(key)
+        ring_b.wait_shared(key)
+
+    ready("own")
+    result = merge(0, jnp.zeros((TOK, 512), F32))
+    for s in (1, 2):
+        ready(("a", s))
+        ready(("b", s))
+        result = merge(-s, merge(s, result))
+    ring_a.take_ahead(4)
+    ready(("a", 3))
+    ready(("b", 3))
+    result = merge(-3, merge(3, result))
+    ring_b.take_ahead(4)
+    ready(("a", 4))
+    out_ref[...] = merge(4, result).astype(BF16)
+
     q_copy(0, 0, me.sibling()).wait_send()
-    kv_copy(kv_in(0), 0, me.sibling(), 1).wait_send()
+    kv_copy(kv_of(0), 0, me.sibling(), 1).wait_send()
 
     @pl.when(p < 3)
     def _():
-        kv_copy(kv_in(0), 0, me.sibling(), 2).wait_send()
+        kv_copy(kv_of(0), 0, me.sibling(), 2).wait_send()
 
     @pl.when(p == 1)
     def _():
-        kv_copy(kv_in(0), 0, me.sibling(), 3).wait_send()
+        kv_copy(kv_of(0), 0, me.sibling(), 3).wait_send()
 
     @pl.when(p == 2)
     def _():
-        kv_copy(kv_in(0), 0, me.sibling(), 3).wait_send()
-        kv_copy(kv_in(0), 0, me.sibling(), 4).wait_send()
+        kv_copy(kv_of(0), 0, me.sibling(), 3).wait_send()
+        kv_copy(kv_of(0), 0, me.sibling(), 4).wait_send()
 
     for b in range(3):
-        share(b, kv_in(0)).wait_send()
+        share(b, kv_of(0)).wait_send()
 
     @pl.when((p == 0) | (p == 3))
     def _():
-        share(3, kv_in(0)).wait_send()
-
-    give.wait()
-
-
-def attend(qkv):
+        share(3, kv_of(0)).wait_send()
+
+    sends.finish()
+
+
+def layer(tokens, wq, wk, wv, wo, down, up, cosine, sine):
+    slots = 120
+    any_spec = pl.BlockSpec(memory_space=pl.ANY)
     vmem = pl.BlockSpec(memory_space=pltpu.VMEM)
     return pl.pallas_call(
-        attend_kernel,
-        out_shape=jax.ShapeDtypeStruct((2, 2 * TOK, HEAD), BF16),
-        in_specs=[pl.BlockSpec(memory_space=pl.ANY)],
+        layer_kernel,
+        out_shape=jax.ShapeDtypeStruct((TOK, 512), BF16),
+        in_specs=[any_spec] * 5 + [vmem] * 4,
         out_specs=vmem,
         scratch_shapes=[
+            pltpu.VMEM((8, 2, TOK, 512), BF16),
+            pltpu.VMEM((3, 8, 2, 2, 128, 256), BF16),
+            pltpu.VMEM((3, 512, 256), F32),
+            pltpu.VMEM((512, 24), F32),
+            pltpu.VMEM((2, 3, 512, HEAD), BF16),
             pltpu.VMEM((2, 512, HEAD), BF16),
             pltpu.VMEM((4, 2, 2, 512, HEAD), BF16),
             pltpu.VMEM((2, 512, HEAD), F32),
             pltpu.VMEM((2, 512, 1), F32),
             pltpu.VMEM((2, 512, 1), F32),
             pltpu.VMEM((2, 512, HEAD), BF16),
-            pltpu.SemaphoreType.DMA((10,)),
-            pltpu.SemaphoreType.DMA((10,)),
-            pltpu.SemaphoreType.DMA((2,)),
+            pltpu.VMEM((8, 4, TOK, HEAD), BF16),
+            pltpu.VMEM((8, 2, 2, 128, 512), BF16),
+            pltpu.SemaphoreType.DMA((slots,)),
+            pltpu.SemaphoreType.DMA((slots,)),
+            pltpu.SemaphoreType.DMA((9,)),
+            pltpu.SemaphoreType.DMA((9,)),
+            pltpu.SemaphoreType.DMA((5,)),
         ],
         compiler_params=pltpu.CompilerParams(
-            collective_id=1, has_side_effects=True, vmem_limit_bytes=40 << 20
+            collective_id=0, has_side_effects=True, vmem_limit_bytes=48 << 20
         ),
-        name="attend",
-    )(qkv)
-
-
-def merge_kernel(
-    heads_in, wo_in, out_ref, merged, weights, acc, stage, send_sem, recv_sem, local_sem
-):
-    me = Place()
-    own_cols = pl.multiple_of(me.xl * 256, 256)
-    other_cols = pl.multiple_of((1 - me.xl) * 256, 256)
-    local = [
-        pltpu.make_async_copy(heads_in, merged.at[me.h, me.xl], local_sem.at[0]),
-        pltpu.make_async_copy(
-            wo_in.at[:, pl.ds(own_cols, 256)], weights.at[me.z, me.xl, me.k], local_sem.at[1]
-        ),
-    ]
-    for copy in local:
-        copy.start()
-    greet(all_neighbours(me))
-    sends = Sends(send_sem, recv_sem)
-    trade = sends.start(
-        wo_in.at[:, pl.ds(other_cols, 256)],
-        weights.at[me.z, me.xl, me.k],
-        me.partner(),
-        sends.slot(),
-    )
-    for copy in local:
-        copy.wait()
-
-    def block(half, x, y):
-        return merged.at[lax.div(x, 2) * 4 + y, lax.rem(x, 2), half]
-
-    events = PlaneGather(sends, me, block).events()
-    ring = RingZ(sends, me, lambda z, k: weights.at[z, :, k])
-    events[0]()
-    trade.wait_recv()
-    ring.start()
-    events[1]()
-    events[2]()
-    ring.take_ahead(1)
-    ring.take_back(1)
-    events[3]()
-    events[4]()
-    ring.take_ahead(2)
-    ring.take_back(2)
-    events[5]()
-    ring.take_ahead(3)
-    ring.take_back(3)
-    events[6]()
-    ring.take_ahead(4)
-    events[7]()
-    ring.wait_shared("own")
-    for s in (1, 2, 3):
-        ring.wait_shared(("a", s))
-        ring.wait_shared(("b", s))
-    ring.wait_shared(("a", 4))
-    events[8]()
-
-    def multiply(h, total):
-        for xl in range(2):
-            left = jnp.concatenate([merged[h, xl, 0], merged[h, xl, 1]], axis=1)
-            total = total + jnp.dot(
-                left, weights[h, xl].reshape(256, 256), preferred_element_type=F32
-            )
-        return total
-
-    acc[...] = jnp.zeros_like(acc)
-
-    @pl.loop(0, 8)
-    def _(h):
-        acc[...] = multiply(h, acc[...])
-
-    stage[0] = acc[pl.ds(0, TOK)].astype(BF16)
-    stage[1] = acc[pl.ds(TOK, TOK)].astype(BF16)
-    give = sends.start(
-        stage.at[1 - me.xl], out_ref.at[:, pl.ds(own_cols, 256)], me.partner(), sends.slot()
-    )
-    out_ref[:, pl.ds(own_cols, 256)] = stage[me.xl]
-    give.wait_recv()
-    sends.finish()
-
-
-def merge(heads, wo):
-    any_spec = pl.BlockSpec(memory_space=pl.ANY)
-    vmem = pl.BlockSpec(memory_space=pltpu.VMEM)
-    return pl.pallas_call(
-        merge_kernel,
-        out_shape=jax.ShapeDtypeStruct((TOK, 512), BF16),
-        in_specs=[any_spec] * 2,
-        out_specs=vmem,
-        scratch_shapes=[
-            pltpu.VMEM((8, 2, 2, 512, HEAD), BF16),
-            pltpu.VMEM((8, 2, 2, 128, 256), BF16),
-            pltpu.VMEM((512, 256), F32),
-            pltpu.VMEM((2, TOK, 256), BF16),
-            pltpu.SemaphoreType.DMA((64,)),
-            pltpu.SemaphoreType.DMA((64,)),
-            pltpu.SemaphoreType.DMA((2,)),
-        ],
-        compiler_params=pltpu.CompilerParams(
-            collective_id=2, has_side_effects=True, vmem_limit_bytes=40 << 20
-        ),
-        name="merge",
-    )(heads, wo)
+        name="layer",
+    )(tokens, wq, wk, wv, wo, down, up, cosine, sine)
 
 
 def rotary_tables():
@@ -687,9 +669,7 @@
 
 def per_device(tokens, wq, wk, wv, wo, down, up):
     cosine, sine = rotary_tables()
-    qkv = project(tokens, wq, wk, wv, down.reshape(24, D), up.reshape(24, 512), cosine, sine)
-    heads = attend(qkv)
-    return merge(heads, wo)
+    return layer(tokens, wq, wk, wv, wo, down.reshape(24, D), up.reshape(24, 512), cosine, sine)
 
 
 def solution(mesh):

time: 132 us -> 116 us (0.88)
  the two profiles are of different devices: /device:TPU:2 before, /device:TPU:1 now
where the time goes in v2:
time: 116 us
  Pallas kernels  113 us (97%)
  local copies, waits for them, and re-layouts  1.68 us (1%)
  other arithmetic  1.22 us (1%)
    pallas_call x1, Pallas kernels, layer(): pl.pallas_call(layer_kernel, out_shape=jax.ShapeDtypeStruct((TOK, 512), B...  113 us

profile of v2, /device:TPU:1, one launch (start us, length us, event | category | flops | bytes accessed | tf_op | source)
XLA Modules:
  0.0 115.8 jit_solution(2146528399208478144)
XLA Ops:
  0.0 1.0 fusion
  1.0 0.0 copy-start
  1.0 0.0 copy-start.1
  1.0 0.0 copy-start.2
  1.1 0.0 copy-start.3
  1.1 0.0 copy-start.4
  1.1 0.0 copy-start.5
  1.1 0.0 copy-start.6
  1.1 0.2 pad_maximum_fusion
  1.3 0.7 copy-done
  2.0 0.1 copy-done.1
  2.0 0.1 copy-done.2
  2.1 0.1 copy-done.3
  2.2 0.0 copy-done.4
  2.2 0.0 copy-done.5
  2.3 0.0 copy-done.6
  2.3 112.8 %layer.1 = bf16[256,512]{1,0:T(8,128)(2,1)S(1)} custom-call(bf16[256,512]{1,0:T(8,128)(2,1)S(1)} %copy-done, bf16[128,512]{1,0:T(8,128)(2,1)S(1)} %copy-done.2, bf16[128,512]{1,0:T(8,128)(2,1)S(1)} %copy-done.3, bf16[128,512]{1,0:T(8,128)(2,1)S(1)} %copy-done.4, bf16[128,512]{1,0:T(8,128)(2,1)S(1)} %copy-done.5, bf16[24,4096]{1,0:T(8,128)(2,1)S(1)} %bitcast.2, ...), custom_call_target="tpu_custom_call" | custom-call | tf_op jit(solution)/shard_map/layer/pallas_call | solution.py:627
  115.1 0.7 copy.9
  (2 shorter events, 0.0 us)
Async XLA Ops:
  1.0 1.0 copy-start
  1.0 1.0 copy-start.1
  1.0 1.1 copy-start.2
  1.1 1.1 copy-start.3
  1.1 1.1 copy-start.4
  1.1 1.2 %copy-start.5 = (bf16[128,512]{1,0:T(8,128)(2,1)S(1)}, bf16[128,512]{1,0:T(8,128)(2,1)}, u32[]{:S(2)}) copy-start(bf16[128,512]{1,0:T(8,128)(2,1)} %wo_in.1) | copy-start | bytes 393220
  1.1 1.2 %copy-start.6 = (bf16[3,8,512]{2,1,0:T(8,128)(2,1)S(1)}, bf16[3,8,512]{2,1,0:T(8,128)(2,1)}, u32[]{:S(2)}) copy-start(bf16[3,8,512]{2,1,0:T(8,128)(2,1)} %param.13) | copy-start | bytes 73732

commit v3 on v2

--- a/solution.py
+++ b/solution.py
@@ -248,7 +248,7 @@
 def layer_kernel(
     tok_in, wq_in, wk_in, wv_in, wo_in, down_ref, up_ref, cos_ref, sin_ref, out_ref,
     tok, weights, acc, low, qkv, query, kv, total, top, denom, heads_out, merged, wo,
-    send_sem, recv_sem, pair_send, pair_recv, local_sem,
+    send_sem, recv_sem, pair_send, pair_recv, hand_send, hand_recv, local_sem,
 ):
     me = Place()
     w_in = (wq_in, wk_in, wv_in)
@@ -256,7 +256,7 @@
     other_cols = pl.multiple_of((1 - me.xl) * 256, 256)
     p = lax.rem(me.z + 8 - 2 * me.xh, 4)
     mine = lax.div(p, 2)
-    lower = p + mine * (3 - 2 * p)
+    last = lax.rem(p, 2)
 
     def plane(q, x=None):
         return me.at(z=lax.rem(me.z + 8 - p + q, 8), x=x)
@@ -275,7 +275,8 @@
     greet(
         [
             me.to_z(1), me.to_z(-1), me.to_x(1), me.to_x(-1), me.to_x(2), me.to_y(1), me.to_y(-1), me.sibling(),
-            plane(lax.rem(p + 1, 4)), plane(lax.rem(p + 2, 4)), plane(lax.rem(p + 3, 4)), plane(3 - p, partner_x),
+            plane(lax.rem(p + 1, 4)), plane(lax.rem(p + 2, 4)), plane(lax.rem(p + 3, 4)),
+            plane(lax.rem(p + 1, 4), partner_x), plane(lax.rem(p + 2, 4), partner_x), plane(lax.rem(p + 3, 4), partner_x),
         ]
     )
     sends = Sends(send_sem, recv_sem)
@@ -358,7 +359,13 @@
     other_ring.take_ahead(3)
     other_ring.take_back(3)
     own_ring.take_ahead(4)
-    low[...] = lax.fori_loop(4, 8, low_rank, low[...])
+    rank = lax.fori_loop(4, 8, low_rank, low[...]).astype(BF16)
+    rank_of = lax.broadcasted_iota(jnp.int32, (512, 24), 1) // 8
+    for j in range(3):
+        part_rank = jnp.where(rank_of == j, rank, jnp.zeros_like(rank))
+        acc[j] += 2.0 * jnp.dot(
+            part_rank, up_ref[:, pl.ds(own_cols, 256)], preferred_element_type=F32
+        )
     shared(("a", 3))
     shared(("b", 3))
     multiply(3)
@@ -369,29 +376,23 @@
     other_ring.take_ahead(4)
     shared(("a", 4))
     multiply(4)
-    rank = low[...].astype(BF16)
-    rank_of = lax.broadcasted_iota(jnp.int32, (512, 24), 1) // 8
 
     def finish_projection(j):
-        part_rank = jnp.where(rank_of == j, rank, jnp.zeros_like(rank))
-        full = acc[j] + 2.0 * jnp.dot(
-            part_rank, up_ref[:, pl.ds(own_cols, 256)], preferred_element_type=F32
-        )
         for head in range(2):
-            part = full[:, head * HEAD : (head + 1) * HEAD]
+            part = acc[j, :, head * HEAD : (head + 1) * HEAD]
             if j < 2:
                 part = part * cos_ref[...] + pltpu.roll(part, HEAD // 2, 1) * sin_ref[...]
             qkv[head, j] = part.astype(BF16)
 
     def kv_copy(src, b, device, send):
         return pltpu.make_async_remote_copy(
-            src, kv.at[b, me.k], pair_send.at[send], pair_recv.at[1 + b],
+            src, kv.at[b, me.k], pair_send.at[send], pair_recv.at[b],
             device_id=device, device_id_type=MESH,
         )
 
-    def q_copy(head, slot, device):
+    def q_copy(head, b, device, send):
         return pltpu.make_async_remote_copy(
-            qkv.at[head, 0], query.at[slot], pair_send.at[0], pair_recv.at[0],
+            qkv.at[head, 0], query.at[b], pair_send.at[send], pair_recv.at[4 + b],
             device_id=device, device_id_type=MESH,
         )
 
@@ -400,7 +401,7 @@
 
     def share(b, src):
         return pltpu.make_async_remote_copy(
-            src, kv.at[b, me.k], pair_send.at[5 + b], pair_recv.at[5 + b],
+            src, kv.at[b, me.k], pair_send.at[8 + b], pair_recv.at[8 + b],
             device_id=me.sibling(), device_id_type=MESH,
         )
 
@@ -410,144 +411,248 @@
     @pl.when(p == 0)
     def _():
         kv_copy(kv_of(0), 0, plane(1), 1).start()
-        kv_copy(kv_of(1), 0, plane(2), 2).start()
 
     @pl.when(p == 1)
     def _():
-        kv_copy(kv_of(1), 1, plane(2), 2).start()
+        kv_copy(kv_of(1), 1, plane(2), 1).start()
 
     @pl.when(p == 2)
     def _():
-        kv_copy(kv_of(0), 2, plane(1), 1).start()
+        kv_copy(kv_of(0), 2, plane(1), 0).start()
+        kv_copy(kv_of(1), 2, plane(3), 1).start()
 
     share(p, kv_of(mine)).start()
     finish_projection(0)
 
-    @pl.when(p == 0)
-    def _():
-        q_copy(1, 0, plane(3)).start()
-
     @pl.when(p == 1)
     def _():
-        q_copy(1, 0, plane(2)).start()
-        kv_copy(kv_of(0), 1, plane(0), 1).start()
-
-    @pl.when(p == 2)
-    def _():
-        q_copy(0, 1, plane(1)).start()
-        kv_copy(kv_of(1), 2, plane(3), 2).start()
-
-    @pl.when(p == 3)
-    def _():
-        q_copy(0, 1, plane(0)).start()
-        kv_copy(kv_of(0), 3, plane(0), 1).start()
-
-    query[mine] = qkv[mine, 0]
+        q_copy(0, 1, plane(0), 2).start()
+        kv_copy(kv_of(0), 1, plane(0), 0).start()
+
+    @pl.when(p != 1)
+    def _():
+        query[p] = qkv[mine, 0]
+
     kv[p, me.k] = qkv[mine, 1:3]
-    rows = lax.broadcasted_iota(jnp.int32, (TOK, 512), 0)
-    cols = lax.broadcasted_iota(jnp.int32, (TOK, 512), 1)
-    key_place = lax.div(cols, 256) * 512 + lax.rem(cols, 256)
-    scale = HEAD ** (-0.5)
-
-    def update(slot, b, half, core, masked):
-        q = query[slot, pl.ds(half * TOK, TOK)]
-        scores = lax.dot_general(
-            q, kv[b, core, 0], (((1,), (1,)), ((), ())), preferred_element_type=F32
-        ) * scale
-        if masked:
-            allowed = key_place + core * 256 <= rows + half * 512 + me.k * 256
-            scores = jnp.where(allowed, scores, -1e30)
-        part = pl.ds(half * TOK, TOK)
-        old = top[slot, part]
-        new = jnp.maximum(old, jnp.max(scores, axis=1, keepdims=True))
-        probs = jnp.exp(scores - new)
-        if masked:
-            probs = jnp.where(allowed, probs, 0.0)
-        factor = jnp.exp(old - new)
-        top[slot, part] = new
-        denom[slot, part] = denom[slot, part] * factor + jnp.sum(probs, axis=1, keepdims=True)
-        total[slot, part] = total[slot, part] * factor + jnp.dot(
-            probs.astype(BF16), kv[b, core, 1], preferred_element_type=F32
-        )
-
-    def block_of(slot):
-        return lower + slot * (3 - 2 * lower)
-
-    def pair(slot, b):
-        @pl.when(block_of(slot) > b)
-        def _():
-            for half in range(2):
-                for core in range(2):
-                    update(slot, b, half, core, False)
-
-        @pl.when(block_of(slot) == b)
-        def _():
-            for half in range(2):
-                for core in range(2):
-                    update(slot, b, half, core, True)
-
-    def step(t, carry):
-        b = jnp.where(
-            p == 0, t, jnp.where(p == 3, 3 - t, jnp.where(p == 1, lax.rem(t + 1, 3), 2 - t))
-        )
-        used = (p == 0) | (p == 3) | (t < 3)
-
-        @pl.when(used & (t > 0))
-        def _():
-            kv_copy(kv.at[b, me.k], b, me.sibling(), 1).wait_recv()
-            share(b, kv.at[b, me.k]).start()
-
-            @pl.when((p == 1) & (b == 2))
-            def _():
-                kv_copy(kv.at[2, me.k], 2, plane(0), 3).start()
-
-            @pl.when(p == 2)
-            def _():
-                kv_copy(kv.at[b, me.k], b, plane(3), 3 + lax.rem(b, 2)).start()
-
-        @pl.when(t == 1)
-        def _():
-            q_copy(0, 1 - mine, me.sibling()).wait_recv()
-
-        @pl.when(used)
-        def _():
-            share(b, kv.at[b, me.k]).wait_recv()
-            first = jnp.where(t == 0, mine, 0)
-            count = jnp.where(t == 0, 1, 2)
-
-            def slots(i, c):
-                pair(first + i, b)
-                return c
-
-            lax.fori_loop(0, count, slots, 0)
-
-            @pl.when((t == 1) & (block_of(1 - mine) >= p))
-            def _():
-                pair(1 - mine, p)
-
-        return carry
-
-    lax.fori_loop(0, 4, step, 0)
-    trade_wo.wait_recv()
     ring_a = RingZ(sends, me, lambda z, k: wo.at[z, me.xl, k])
     ring_b = RingZ(sends, me, lambda z, k: wo.at[z, 1 - me.xl, k])
-    give = []
+    scale = HEAD ** (-0.5)
+
+    def allowed(half, core, keys):
+        rows = lax.broadcasted_iota(jnp.int32, (TOK, keys), 0)
+        cols = lax.broadcasted_iota(jnp.int32, (TOK, keys), 1)
+        place = cols + jnp.where(cols >= TOK, 256, 0)
+        return place + core * 256 <= rows + half * 512 + me.k * 256
+
+    def pair(slot, b, diagonal):
+        for half in range(2):
+            part = pl.ds(half * TOK, TOK)
+            keys = TOK if diagonal and half == 0 else 2 * TOK
+            q = query[slot, part]
+            scores = []
+            for core in range(2):
+                score = lax.dot_general(
+                    q, kv[b, core, 0, pl.ds(0, keys)], (((1,), (1,)), ((), ())), preferred_element_type=F32
+                ) * scale
+                if diagonal:
+                    score = jnp.where(allowed(half, core, keys), score, -1e30)
+                scores.append(score)
+            old = top[slot, part]
+            new = jnp.maximum(old, jnp.max(jnp.maximum(scores[0], scores[1]), axis=1, keepdims=True))
+            probs = [jnp.exp(score - new) for score in scores]
+            if diagonal:
+                probs = [
+                    jnp.where(allowed(half, core, keys), probs[core], 0.0) for core in range(2)
+                ]
+            factor = jnp.exp(old - new)
+            top[slot, part] = new
+            denom[slot, part] = denom[slot, part] * factor + jnp.sum(
+                probs[0] + probs[1], axis=1, keepdims=True
+            )
+            result = total[slot, part] * factor
+            for core in range(2):
+                result = result + jnp.dot(
+                    probs[core].astype(BF16),
+                    kv[b, core, 1, pl.ds(0, keys)],
+                    preferred_element_type=F32,
+                )
+            total[slot, part] = result
+
+    def arrive(b, onward=None):
+        kv_copy(kv.at[b, me.k], b, me.sibling(), 0).wait_recv()
+        if onward is not None:
+            kv_copy(kv.at[b, me.k], b, plane(onward), 4 + b).start()
+        share(b, kv.at[b, me.k]).start()
+
+    def got_query(b):
+        q_copy(0, b, me.sibling(), 2).wait_recv()
+
+    def whole(b):
+        share(b, kv.at[b, me.k]).wait_recv()
+
+    def pairs(first, count, b):
+        def one(i, c):
+            pair(first + i, b, False)
+            return c
+
+        lax.fori_loop(0, count, one, 0)
+
+    whole(p)
+
+    @pl.when(p != 1)
+    def _():
+        pair(p, p, True)
+
+    one = 1 + last
+
+    @pl.when(p == 0)
+    def _():
+        kv_copy(kv_of(0), 0, me.sibling(), 1).wait_send()
+        kv_copy(kv_of(1), 0, plane(2), 0).start()
+        arrive(1)
+        got_query(1)
+
+    @pl.when(p == 1)
+    def _():
+        arrive(2, 0)
+        got_query(3)
+        q_copy(1, 1, plane(2), 3).start()
+
+    @pl.when(p == 2)
+    def _():
+        arrive(1, 3)
+        kv_copy(kv_of(0), 2, me.sibling(), 0).wait_send()
+        q_copy(0, 2, plane(0), 2).start()
+
+    @pl.when(p == 3)
+    def _():
+        arrive(2)
+        q_copy(0, 3, plane(1), 2).start()
+        kv_copy(kv_of(0), 3, plane(1), 0).start()
+
+    whole(one)
+
+    @pl.when(p == 0)
+    def _():
+        pair(1, 1, True)
+
+    def second(i, c):
+        q = jnp.where(p == 0, 1, jnp.where(p == 2, 2, 3))
+        b = jnp.where(p == 0, 0, jnp.where(p == 1, 1 + i, jnp.where(p == 2, 1, 2)))
+        pair(q, b, False)
+        return c
+
+    lax.fori_loop(0, jnp.where(p == 1, 2, 1), second, 0)
+
+    @pl.when(p == 0)
+    def _():
+        kv_copy(kv_of(1), 0, me.sibling(), 0).wait_send()
+        q_copy(1, 0, plane(2), 2).start()
+        got_query(2)
+
+    @pl.when(p == 1)
+    def _():
+        arrive(0)
+
+    @pl.when(p == 2)
+    def _():
+        arrive(0, 3)
+        got_query(1)
+
+    @pl.when(p == 3)
+    def _():
+        arrive(1)
+
+    @pl.when(p != 0)
+    def _():
+        whole(jnp.where(p == 3, 1, 0))
+
+    def third(i, c):
+        q = jnp.where(p == 0, 2, jnp.where(p == 2, 1 + i, 3))
+        b = jnp.where(p == 0, i, jnp.where(p == 3, 1, 0))
+        pair(q, b, False)
+        return c
+
+    lax.fori_loop(0, 2 - last, third, 0)
+
+    @pl.when(p == 0)
+    def _():
+        arrive(2)
+        whole(2)
+
+    @pl.when(p == 1)
+    def _():
+        arrive(3)
+        whole(3)
+
+    @pl.when(p == 2)
+    def _():
+        got_query(0)
+
+    def own_keys(i, c):
+        q = jnp.where(p == 0, 2, jnp.where(p == 1, 3, 1 - i))
+        pair(q, q, True)
+        return c
+
+    @pl.when(p != 3)
+    def _():
+        lax.fori_loop(0, jnp.where(p == 2, 2, 1), own_keys, 0)
+
+    @pl.when(p == 3)
+    def _():
+        arrive(0)
+        whole(0)
+        pair(3, 0, False)
+
+    def rows_of(r):
+        return pl.ds(pl.multiple_of(r * TOK, TOK), TOK)
+
     place = merged.at[me.h, me.xl * 2 + mine]
 
-    far_slot = 1 - mine
-    heads_out[far_slot] = (total[far_slot] / denom[far_slot]).astype(BF16)
-    for x, r in ((me.x, me.xl), (partner_x, 1 - me.xl)):
-        rows_r = pl.ds(pl.multiple_of(r * TOK, TOK), TOK)
-        give.append(sends.start(heads_out.at[far_slot, rows_r], place, plane(3 - p, x), sends.slot()))
-    heads_out[mine] = (total[mine] / denom[mine]).astype(BF16)
-    rows_r = pl.ds(pl.multiple_of((1 - me.xl) * TOK, TOK), TOK)
-    give.append(sends.start(heads_out.at[mine, rows_r], place, me.partner(), sends.slot()))
-    merged[me.h, me.xl * 2 + mine] = heads_out[mine, pl.ds(pl.multiple_of(me.xl * TOK, TOK), TOK)]
+    def hand_copy(b, r, x, column):
+        return pltpu.make_async_remote_copy(
+            heads_out.at[b, rows_of(r)], place, hand_send.at[2 * b + column], hand_recv.at[2 * mine + column],
+            device_id=plane(b, x), device_id_type=MESH,
+        )
+
+    def hand_over(b):
+        heads_out[b] = (total[b] / denom[b]).astype(BF16)
+        hand_copy(b, 1 - me.xl, partner_x, 1).start()
+
+        @pl.when(b != p)
+        def _():
+            hand_copy(b, me.xl, me.x, 0).start()
+
+        @pl.when(b == p)
+        def _():
+            merged[me.h, me.xl * 2 + mine] = heads_out[p, rows_of(me.xl)]
+
+    @pl.when(last == 1)
+    def _():
+        hand_over(3)
+
+    @pl.when(last == 0)
+    def _():
+        for b in (1, 0, 2):
+            hand_over(b)
+
+    trade_wo.wait_recv()
     ring_a.start()
     ring_b.start()
-
-    for copy in give:
-        copy.wait_recv()
+    for head in range(2):
+        pltpu.make_async_remote_copy(
+            heads_out.at[0, pl.ds(0, TOK)], place, hand_send.at[0], hand_recv.at[2 * head + 1],
+            device_id=me.sibling(), device_id_type=MESH,
+        ).wait_recv()
+        here = (p == 0) if head == 0 else (p >= 2)
+
+        @pl.when(jnp.logical_not(here))
+        def _():
+            pltpu.make_async_remote_copy(
+                heads_out.at[0, pl.ds(0, TOK)], place, hand_send.at[0], hand_recv.at[2 * head],
+                device_id=me.sibling(), device_id_type=MESH,
+            ).wait_recv()
+
     gather = HeadGather(sends, me, lambda half, xh, y: merged.at[xh * 4 + y, pl.ds(half * 2, 2)])
     gather.start()
     ring_a.take_ahead(1)
@@ -594,28 +699,46 @@
     ready(("a", 4))
     out_ref[...] = merge(4, result).astype(BF16)
 
-    q_copy(0, 0, me.sibling()).wait_send()
-    kv_copy(kv_of(0), 0, me.sibling(), 1).wait_send()
-
-    @pl.when(p < 3)
-    def _():
-        kv_copy(kv_of(0), 0, me.sibling(), 2).wait_send()
+    q_copy(0, 0, me.sibling(), 2).wait_send()
+
+    @pl.when(last == 1)
+    def _():
+        kv_copy(kv_of(0), 0, me.sibling(), 0).wait_send()
+
+    @pl.when((p == 1) | (p == 2))
+    def _():
+        kv_copy(kv_of(0), 0, me.sibling(), 1).wait_send()
 
     @pl.when(p == 1)
     def _():
-        kv_copy(kv_of(0), 0, me.sibling(), 3).wait_send()
+        q_copy(0, 0, me.sibling(), 3).wait_send()
+        kv_copy(kv_of(0), 0, me.sibling(), 6).wait_send()
 
     @pl.when(p == 2)
     def _():
-        kv_copy(kv_of(0), 0, me.sibling(), 3).wait_send()
         kv_copy(kv_of(0), 0, me.sibling(), 4).wait_send()
+        kv_copy(kv_of(0), 0, me.sibling(), 5).wait_send()
 
     for b in range(3):
         share(b, kv_of(0)).wait_send()
 
-    @pl.when((p == 0) | (p == 3))
+    @pl.when(last == 1)
     def _():
         share(3, kv_of(0)).wait_send()
+        hand_copy(3, 0, partner_x, 1).wait_send()
+
+    @pl.when(p == 1)
+    def _():
+        hand_copy(3, 0, me.x, 0).wait_send()
+
+    @pl.when(last == 0)
+    def _():
+        for b in range(3):
+            hand_copy(b, 0, partner_x, 1).wait_send()
+
+            @pl.when(b != p)
+            def _():
+                hand_copy(b, 0, me.x, 0).wait_send()
 
     sends.finish()
 
@@ -635,18 +758,20 @@
             pltpu.VMEM((3, 512, 256), F32),
             pltpu.VMEM((512, 24), F32),
             pltpu.VMEM((2, 3, 512, HEAD), BF16),
-            pltpu.VMEM((2, 512, HEAD), BF16),
+            pltpu.VMEM((4, 512, HEAD), BF16),
             pltpu.VMEM((4, 2, 2, 512, HEAD), BF16),
-            pltpu.VMEM((2, 512, HEAD), F32),
-            pltpu.VMEM((2, 512, 1), F32),
-            pltpu.VMEM((2, 512, 1), F32),
-            pltpu.VMEM((2, 512, HEAD), BF16),
+            pltpu.VMEM((4, 512, HEAD), F32),
+            pltpu.VMEM((4, 512, 1), F32),
+            pltpu.VMEM((4, 512, 1), F32),
+            pltpu.VMEM((4, 512, HEAD), BF16),
             pltpu.VMEM((8, 4, TOK, HEAD), BF16),
             pltpu.VMEM((8, 2, 2, 128, 512), BF16),
             pltpu.SemaphoreType.DMA((slots,)),
             pltpu.SemaphoreType.DMA((slots,)),
-            pltpu.SemaphoreType.DMA((9,)),
-            pltpu.SemaphoreType.DMA((9,)),
+            pltpu.SemaphoreType.DMA((12,)),
+            pltpu.SemaphoreType.DMA((12,)),
+            pltpu.SemaphoreType.DMA((8,)),
+            pltpu.SemaphoreType.DMA((4,)),
             pltpu.SemaphoreType.DMA((5,)),
         ],
         compiler_params=pltpu.CompilerParams(

time: 116 us -> 110 us (0.948)
  Pallas kernels: 113 us -> 107 us
    pallas_call x1, Pallas kernels: 113 us -> 107 us  [layer(): pl.pallas_call(layer_kernel, out_shape=jax.ShapeDtypeStruct((TOK, 512), B...]
where the time goes in v3:
time: 110 us
  Pallas kernels  107 us (97%)
  local copies, waits for them, and re-layouts  1.68 us (2%)
  other arithmetic  1.22 us (1%)
    pallas_call x1, Pallas kernels, layer(): pl.pallas_call(layer_kernel, out_shape=jax.ShapeDtypeStruct((TOK, 512), B...  107 us

profile of v3, /device:TPU:1, one launch (start us, length us, event | category | flops | bytes accessed | tf_op | source)
XLA Modules:
  0.0 110.0 jit_solution(1576890151603191372)
XLA Ops:
  0.0 1.0 fusion
  1.0 0.0 copy-start
  1.0 0.0 copy-start.1
  1.0 0.0 copy-start.2
  1.1 0.0 copy-start.3
  1.1 0.0 copy-start.4
  1.1 0.0 copy-start.5
  1.1 0.0 copy-start.6
  1.1 0.2 pad_maximum_fusion
  1.3 0.7 copy-done
  2.0 0.1 copy-done.1
  2.0 0.1 copy-done.2
  2.1 0.1 copy-done.3
  2.2 0.0 copy-done.4
  2.2 0.0 copy-done.5
  2.3 0.0 copy-done.6
  2.3 107.0 %layer.1 = bf16[256,512]{1,0:T(8,128)(2,1)S(1)} custom-call(bf16[256,512]{1,0:T(8,128)(2,1)S(1)} %copy-done, bf16[128,512]{1,0:T(8,128)(2,1)S(1)} %copy-done.2, bf16[128,512]{1,0:T(8,128)(2,1)S(1)} %copy-done.3, bf16[128,512]{1,0:T(8,128)(2,1)S(1)} %copy-done.4, bf16[128,512]{1,0:T(8,128)(2,1)S(1)} %copy-done.5, bf16[24,4096]{1,0:T(8,128)(2,1)S(1)} %bitcast.2, ...), custom_call_target="tpu_custom_call" | custom-call | tf_op jit(solution)/shard_map/layer/pallas_call | solution.py:750
  109.3 0.7 copy.9
  (2 shorter events, 0.0 us)
Async XLA Ops:
  1.0 1.0 copy-start
  1.0 1.0 copy-start.1
  1.0 1.1 copy-start.2
  1.1 1.1 %copy-start.3 = (bf16[128,512]{1,0:T(8,128)(2,1)S(1)}, bf16[128,512]{1,0:T(8,128)(2,1)}, u32[]{:S(2)}) copy-start(bf16[128,512]{1,0:T(8,128)(2,1)} %wk_in.1) | copy-start | bytes 393220
  1.1 1.1 %copy-start.4 = (bf16[128,512]{1,0:T(8,128)(2,1)S(1)}, bf16[128,512]{1,0:T(8,128)(2,1)}, u32[]{:S(2)}) copy-start(bf16[128,512]{1,0:T(8,128)(2,1)} %wv_in.1) | copy-start | bytes 393220
  1.1 1.2 %copy-start.5 = (bf16[128,512]{1,0:T(8,128)(2,1)S(1)}, bf16[128,512]{1,0:T(8,128)(2,1)}, u32[]{:S(2)}) copy-start(bf16[128,512]{1,0:T(8,128)(2,1)} %wo_in.1) | copy-start | bytes 393220
  1.1 1.2 %copy-start.6 = (bf16[3,8,512]{2,1,0:T(8,128)(2,1)S(1)}, bf16[3,8,512]{2,1,0:T(8,128)(2,1)}, u32[]{:S(2)}) copy-start(bf16[3,8,512]{2,1,0:T(8,128)(2,1)} %param.13) | copy-start | bytes 73732

commit v4 on v3

--- a/solution.py
+++ b/solution.py
@@ -2,6 +2,7 @@
 
 import jax
 import jax.numpy as jnp
+import numpy as np
 from jax import lax
 from jax.experimental import pallas as pl
 from jax.experimental.pallas import tpu as pltpu
@@ -246,8 +247,8 @@
 
 
 def layer_kernel(
-    tok_in, wq_in, wk_in, wv_in, wo_in, down_ref, up_ref, cos_ref, sin_ref, out_ref,
-    tok, weights, acc, low, qkv, query, kv, total, top, denom, heads_out, merged, wo,
+    tok_in, wq_in, wk_in, wv_in, wo_in, down_in, up_in, angle_in, out_ref,
+    down_ref, up_ref, angles, turn, tok, weights, acc, low, qkv, query, kv, total, top, denom, heads_out, merged, wo,
     send_sem, recv_sem, pair_send, pair_recv, hand_send, hand_recv, local_sem,
 ):
     me = Place()
@@ -270,6 +271,9 @@
             )
         )
     local.append(pltpu.make_async_copy(wo_in, wo.at[me.z, me.xl, me.k], local_sem.at[4]))
+    local.append(pltpu.make_async_copy(down_in, down_ref, local_sem.at[5]))
+    local.append(pltpu.make_async_copy(up_in, up_ref, local_sem.at[6]))
+    local.append(pltpu.make_async_copy(angle_in, angles, local_sem.at[7]))
     for copy in local:
         copy.start()
     greet(
@@ -321,6 +325,8 @@
     other_ring.take_ahead(2)
     other_ring.take_back(2)
     events[8]()
+    own_ring.take_ahead(3)
+    own_ring.take_back(3)
     trade_wo = sends.start(
         wo.at[me.z, me.xl, me.k], wo.at[me.z, me.xl, me.k], me.partner(), sends.slot()
     )
@@ -335,6 +341,15 @@
             else:
                 acc[j] += part
 
+    for half in range(2):
+        block_row = 256 + me.z * 4 + half * 2 + me.k
+        block_cos, block_sin = angles[0, pl.ds(block_row, 1)], angles[1, pl.ds(block_row, 1)]
+        row_cos, row_sin = angles[0, pl.ds(0, TOK)], angles[1, pl.ds(0, TOK)]
+        turn[0, pl.ds(half * TOK, TOK)] = row_cos * block_cos - row_sin * block_sin
+        lane = lax.broadcasted_iota(jnp.int32, (TOK, HEAD), 1)
+        sine = row_sin * block_cos + row_cos * block_sin
+        turn[1, pl.ds(half * TOK, TOK)] = jnp.where(lane < HEAD // 2, -sine, sine)
+
     def low_rank(chunk, so_far):
         left = tok[chunk].reshape(512, 512)
         cols = pl.multiple_of(chunk * 512, 512)
@@ -349,16 +364,16 @@
     shared("own")
     multiply(0, True)
     low[...] = lax.fori_loop(0, 4, low_rank, jnp.zeros((512, 24), F32))
-    own_ring.take_ahead(3)
-    own_ring.take_back(3)
-    for s in (1, 2):
-        shared(("a", s))
-        shared(("b", s))
-        multiply(s)
-        multiply(-s)
+    shared(("a", 1))
+    shared(("b", 1))
+    multiply(1)
+    multiply(-1)
     other_ring.take_ahead(3)
     other_ring.take_back(3)
-    own_ring.take_ahead(4)
+    shared(("a", 2))
+    shared(("b", 2))
+    multiply(2)
+    multiply(-2)
     rank = lax.fori_loop(4, 8, low_rank, low[...]).astype(BF16)
     rank_of = lax.broadcasted_iota(jnp.int32, (512, 24), 1) // 8
     for j in range(3):
@@ -366,6 +381,7 @@
         acc[j] += 2.0 * jnp.dot(
             part_rank, up_ref[:, pl.ds(own_cols, 256)], preferred_element_type=F32
         )
+    own_ring.take_ahead(4)
     shared(("a", 3))
     shared(("b", 3))
     multiply(3)
@@ -381,7 +397,7 @@
         for head in range(2):
             part = acc[j, :, head * HEAD : (head + 1) * HEAD]
             if j < 2:
-                part = part * cos_ref[...] + pltpu.roll(part, HEAD // 2, 1) * sin_ref[...]
+                part = part * turn[0] + pltpu.roll(part, HEAD // 2, 1) * turn[1]
             qkv[head, j] = part.astype(BF16)
 
     def kv_copy(src, b, device, send):
@@ -478,6 +494,29 @@
                 )
             total[slot, part] = result
 
+    def rows_of(r):
+        return pl.ds(pl.multiple_of(r * TOK, TOK), TOK)
+
+    place = merged.at[me.h, me.xl * 2 + mine]
+
+    def hand_copy(b, r, x, column):
+        return pltpu.make_async_remote_copy(
+            heads_out.at[b, rows_of(r)], place, hand_send.at[2 * b + column], hand_recv.at[2 * mine + column],
+            device_id=plane(b, x), device_id_type=MESH,
+        )
+
+    def hand_over(b):
+        heads_out[b] = (total[b] / denom[b]).astype(BF16)
+        hand_copy(b, 1 - me.xl, partner_x, 1).start()
+
+        @pl.when(b != p)
+        def _():
+            hand_copy(b, me.xl, me.x, 0).start()
+
+        @pl.when(b == p)
+        def _():
+            merged[me.h, me.xl * 2 + mine] = heads_out[p, rows_of(me.xl)]
+
     def arrive(b, onward=None):
         kv_copy(kv.at[b, me.k], b, me.sibling(), 0).wait_recv()
         if onward is not None:
@@ -546,6 +585,8 @@
 
     @pl.when(p == 0)
     def _():
+        hand_over(1)
+        hand_over(0)
         kv_copy(kv_of(1), 0, me.sibling(), 0).wait_send()
         q_copy(1, 0, plane(2), 2).start()
         got_query(2)
@@ -567,6 +608,8 @@
     def _():
         whole(jnp.where(p == 3, 1, 0))
 
+    trade_wo.wait_recv()
+    ring_a.start()
     def third(i, c):
         q = jnp.where(p == 0, 2, jnp.where(p == 2, 1 + i, 3))
         b = jnp.where(p == 0, i, jnp.where(p == 3, 1, 0))
@@ -587,16 +630,15 @@
 
     @pl.when(p == 2)
     def _():
+        hand_over(2)
+        pair(1, 1, True)
+        hand_over(1)
         got_query(0)
 
-    def own_keys(i, c):
-        q = jnp.where(p == 0, 2, jnp.where(p == 1, 3, 1 - i))
+    @pl.when(p != 3)
+    def _():
+        q = jnp.where(p == 0, 2, jnp.where(p == 1, 3, 0))
         pair(q, q, True)
-        return c
-
-    @pl.when(p != 3)
-    def _():
-        lax.fori_loop(0, jnp.where(p == 2, 2, 1), own_keys, 0)
 
     @pl.when(p == 3)
     def _():
@@ -604,40 +646,18 @@
         whole(0)
         pair(3, 0, False)
 
-    def rows_of(r):
-        return pl.ds(pl.multiple_of(r * TOK, TOK), TOK)
-
-    place = merged.at[me.h, me.xl * 2 + mine]
-
-    def hand_copy(b, r, x, column):
-        return pltpu.make_async_remote_copy(
-            heads_out.at[b, rows_of(r)], place, hand_send.at[2 * b + column], hand_recv.at[2 * mine + column],
-            device_id=plane(b, x), device_id_type=MESH,
-        )
-
-    def hand_over(b):
-        heads_out[b] = (total[b] / denom[b]).astype(BF16)
-        hand_copy(b, 1 - me.xl, partner_x, 1).start()
-
-        @pl.when(b != p)
-        def _():
-            hand_copy(b, me.xl, me.x, 0).start()
-
-        @pl.when(b == p)
-        def _():
-            merged[me.h, me.xl * 2 + mine] = heads_out[p, rows_of(me.xl)]
+    @pl.when(p == 0)
+    def _():
+        hand_over(2)
+
+    @pl.when(p == 2)
+    def _():
+        hand_over(0)
 
     @pl.when(last == 1)
     def _():
         hand_over(3)
 
-    @pl.when(last == 0)
-    def _():
-        for b in (1, 0, 2):
-            hand_over(b)
-
-    trade_wo.wait_recv()
-    ring_a.start()
     ring_b.start()
     for head in range(2):
         pltpu.make_async_remote_copy(
@@ -657,15 +677,15 @@
     gather.start()
     ring_a.take_ahead(1)
     ring_a.take_back(1)
-    gather.step_1()
     ring_b.take_ahead(1)
     ring_b.take_back(1)
+    gather.step_1()
     gather.step_2()
     ring_a.take_ahead(2)
     ring_a.take_back(2)
-    gather.step_3()
     ring_b.take_ahead(2)
     ring_b.take_back(2)
+    gather.step_3()
     ring_a.take_ahead(3)
     ring_a.take_back(3)
     ring_b.take_ahead(3)
@@ -743,16 +763,20 @@
     sends.finish()
 
 
-def layer(tokens, wq, wk, wv, wo, down, up, cosine, sine):
+def layer(tokens, wq, wk, wv, wo, down, up, angles):
     slots = 120
     any_spec = pl.BlockSpec(memory_space=pl.ANY)
     vmem = pl.BlockSpec(memory_space=pltpu.VMEM)
     return pl.pallas_call(
         layer_kernel,
         out_shape=jax.ShapeDtypeStruct((TOK, 512), BF16),
-        in_specs=[any_spec] * 5 + [vmem] * 4,
+        in_specs=[any_spec] * 8,
         out_specs=vmem,
         scratch_shapes=[
+            pltpu.VMEM((24, D), BF16),
+            pltpu.VMEM((24, 512), BF16),
+            pltpu.VMEM((2, 288, HEAD), F32),
+            pltpu.VMEM((2, 512, HEAD), F32),
             pltpu.VMEM((8, 2, TOK, 512), BF16),
             pltpu.VMEM((3, 8, 2, 2, 128, 256), BF16),
             pltpu.VMEM((3, 512, 256), F32),
@@ -772,29 +796,24 @@
             pltpu.SemaphoreType.DMA((12,)),
             pltpu.SemaphoreType.DMA((8,)),
             pltpu.SemaphoreType.DMA((4,)),
-            pltpu.SemaphoreType.DMA((5,)),
+            pltpu.SemaphoreType.DMA((8,)),
         ],
         compiler_params=pltpu.CompilerParams(
-            collective_id=0, has_side_effects=True, vmem_limit_bytes=48 << 20
+            collective_id=0, has_side_effects=True, vmem_limit_bytes=60 << 20
         ),
         name="layer",
-    )(tokens, wq, wk, wv, wo, down, up, cosine, sine)
+    )(tokens, wq, wk, wv, wo, down, up, angles)
 
 
 def rotary_tables():
-    c = lax.axis_index("ctx")
-    base = lax.div(c, 4) * 1024 + lax.rem(c, 2) * 256
-    rows = jnp.arange(512, dtype=jnp.int32)
-    positions = base + (rows // 256) * 512 + rows % 256
-    inverse_freq = 10000.0 ** (-(jnp.arange(HEAD // 2, dtype=F32) * 2.0) / HEAD)
-    angles = positions.astype(F32)[:, None] * inverse_freq[None, :]
-    cosine, sine = jnp.cos(angles), jnp.sin(angles)
-    return jnp.concatenate([cosine, cosine], 1), jnp.concatenate([-sine, sine], 1)
+    rows = np.concatenate([np.arange(TOK), np.arange(32) * TOK]).astype(np.float64)
+    inverse_freq = 10000.0 ** (-(np.arange(HEAD // 2) * 2.0) / HEAD)
+    angle = rows[:, None] * np.concatenate([inverse_freq, inverse_freq])[None, :]
+    return np.stack([np.cos(angle), np.sin(angle)]).astype(np.float32)
 
 
 def per_device(tokens, wq, wk, wv, wo, down, up):
-    cosine, sine = rotary_tables()
-    return layer(tokens, wq, wk, wv, wo, down.reshape(24, D), up.reshape(24, 512), cosine, sine)
+    return layer(tokens, wq, wk, wv, wo, down.reshape(24, D), up.reshape(24, 512), jnp.asarray(rotary_tables()))
 
 
 def solution(mesh):

time: 110 us -> 106 us (0.964)
  Pallas kernels: 107 us -> 103 us
  other arithmetic: 1.22 us -> 0 us
    pallas_call x1, Pallas kernels: 107 us -> 103 us  [layer(): pl.pallas_call(layer_kernel, out_shape=jax.ShapeDtypeStruct((TOK, 512), B...]
where the time goes in v4:
time: 106 us; the launch traced here: 105 us
  Pallas kernels  103 us (97%)
  local copies, waits for them, and re-layouts  1.67 us (2%)
    pallas_call x1, Pallas kernels, layer(): pl.pallas_call(layer_kernel, out_shape=jax.ShapeDtypeStruct((TOK, 512), B...  103 us

profile of v4, /device:TPU:1, one launch (start us, length us, event | category | flops | bytes accessed | tf_op | source)
XLA Modules:
  0.0 105.1 jit_solution(9156619504158445240)
XLA Ops:
  0.0 103.4 %layer.1 = bf16[256,512]{1,0:T(8,128)(2,1)} custom-call(bf16[256,512]{1,0:T(8,128)(2,1)} %tok_in.1, bf16[128,512]{1,0:T(8,128)(2,1)} %wq_in.1, bf16[128,512]{1,0:T(8,128)(2,1)} %wk_in.1, bf16[128,512]{1,0:T(8,128)(2,1)} %wv_in.1, bf16[128,512]{1,0:T(8,128)(2,1)} %wo_in.1, bf16[24,4096]{1,0:T(8,128)(2,1)} %bitcast.2, bf16[24,512]{1,0:T(8,128)(2,1)} %bitcast.3, ...), custom_call_target="tpu_custom_call" | custom-call | tf_op jit(solution)/shard_map/layer/pallas_call | solution.py:770
  103.4 1.7 %copy.10 = bf16[256,512]{1,0:T(8,128)(2,1)} copy(bf16[256,512]{1,0:T(8,128)(2,1)} %layer.1) | data formatting | bytes 524288

commit v5 on v4

--- a/solution.py
+++ b/solution.py
@@ -178,11 +178,13 @@
             self.sends.start(block, block, self.me.to_x(2), self.sends.slot())
         )
 
-    def start(self):
+    def start_a(self):
         self.cross(0, 0)
+        self.own_a.start()
+
+    def start_b(self):
         self.own_b.start()
         self.cross(1, 0)
-        self.own_a.start()
 
     def step_1(self):
         self.own_b.forward()
@@ -497,7 +499,7 @@
     def rows_of(r):
         return pl.ds(pl.multiple_of(r * TOK, TOK), TOK)
 
-    place = merged.at[me.h, me.xl * 2 + mine]
+    place = merged.at[me.h, mine, me.xl]
 
     def hand_copy(b, r, x, column):
         return pltpu.make_async_remote_copy(
@@ -515,7 +517,7 @@
 
         @pl.when(b == p)
         def _():
-            merged[me.h, me.xl * 2 + mine] = heads_out[p, rows_of(me.xl)]
+            merged[me.h, mine, me.xl] = heads_out[p, rows_of(me.xl)]
 
     def arrive(b, onward=None):
         kv_copy(kv.at[b, me.k], b, me.sibling(), 0).wait_recv()
@@ -658,25 +660,30 @@
     def _():
         hand_over(3)
 
-    ring_b.start()
-    for head in range(2):
+    def handed(head, column):
         pltpu.make_async_remote_copy(
-            heads_out.at[0, pl.ds(0, TOK)], place, hand_send.at[0], hand_recv.at[2 * head + 1],
+            heads_out.at[0, pl.ds(0, TOK)], place, hand_send.at[0], hand_recv.at[2 * head + column],
             device_id=me.sibling(), device_id_type=MESH,
         ).wait_recv()
-        here = (p == 0) if head == 0 else (p >= 2)
-
-        @pl.when(jnp.logical_not(here))
-        def _():
-            pltpu.make_async_remote_copy(
-                heads_out.at[0, pl.ds(0, TOK)], place, hand_send.at[0], hand_recv.at[2 * head],
-                device_id=me.sibling(), device_id_type=MESH,
-            ).wait_recv()
-
-    gather = HeadGather(sends, me, lambda half, xh, y: merged.at[xh * 4 + y, pl.ds(half * 2, 2)])
-    gather.start()
+
+    def block_out(half, xh, y):
+        early = lax.div(lax.rem(me.z + 8 - 2 * xh, 4), 2)
+        return merged.at[xh * 4 + y, early + half * (1 - 2 * early)]
+
+    gather = HeadGather(sends, me, block_out)
+    ring_b.start()
+
+    @pl.when(p == 1)
+    def _():
+        handed(mine, 0)
+
+    handed(mine, 1)
+    gather.start_a()
     ring_a.take_ahead(1)
     ring_a.take_back(1)
+    handed(1 - mine, 0)
+    handed(1 - mine, 1)
+    gather.start_b()
     ring_b.take_ahead(1)
     ring_b.take_back(1)
     gather.step_1()
@@ -695,7 +702,7 @@
     def merge(step, so_far):
         h = lax.rem(me.z + 8 + step, 8)
         for half in range(2):
-            left = jnp.concatenate([merged[h, 2 * half], merged[h, 2 * half + 1]], axis=1)
+            left = jnp.concatenate([merged[h, 0, half], merged[h, 1, half]], axis=1)
             so_far = so_far + jnp.dot(
                 left, wo[h, half].reshape(256, 512), preferred_element_type=F32
             )
@@ -788,7 +795,7 @@
             pltpu.VMEM((4, 512, 1), F32),
             pltpu.VMEM((4, 512, 1), F32),
             pltpu.VMEM((4, 512, HEAD), BF16),
-            pltpu.VMEM((8, 4, TOK, HEAD), BF16),
+            pltpu.VMEM((8, 2, 2, TOK, HEAD), BF16),
             pltpu.VMEM((8, 2, 2, 128, 512), BF16),
             pltpu.SemaphoreType.DMA((slots,)),
             pltpu.SemaphoreType.DMA((slots,)),

time: 106 us -> 104 us (0.981)
    pallas_call x1, Pallas kernels: 103 us -> 102 us  [layer(): pl.pallas_call(layer_kernel, out_shape=jax.ShapeDtypeStruct((TOK, 512), B...]
where the time goes in v5:
time: 104 us
  Pallas kernels  102 us (98%)
  local copies, waits for them, and re-layouts  1.67 us (2%)
    pallas_call x1, Pallas kernels, layer(): pl.pallas_call(layer_kernel, out_shape=jax.ShapeDtypeStruct((TOK, 512), B...  102 us

profile of v5, /device:TPU:1, one launch (start us, length us, event | category | flops | bytes accessed | tf_op | source)
XLA Modules:
  0.0 103.8 jit_solution(5209925027530116669)
XLA Ops:
  0.0 102.1 %layer.1 = bf16[256,512]{1,0:T(8,128)(2,1)} custom-call(bf16[256,512]{1,0:T(8,128)(2,1)} %tok_in.1, bf16[128,512]{1,0:T(8,128)(2,1)} %wq_in.1, bf16[128,512]{1,0:T(8,128)(2,1)} %wk_in.1, bf16[128,512]{1,0:T(8,128)(2,1)} %wv_in.1, bf16[128,512]{1,0:T(8,128)(2,1)} %wo_in.1, bf16[24,4096]{1,0:T(8,128)(2,1)} %bitcast.2, bf16[24,512]{1,0:T(8,128)(2,1)} %bitcast.3, ...), custom_call_target="tpu_custom_call" | custom-call | tf_op jit(solution)/shard_map/layer/pallas_call | solution.py:777
  102.1 1.7 %copy.10 = bf16[256,512]{1,0:T(8,128)(2,1)} copy(bf16[256,512]{1,0:T(8,128)(2,1)} %layer.1) | data formatting | bytes 524288

commit v6 on v5

--- a/solution.py
+++ b/solution.py
@@ -333,10 +333,10 @@
         wo.at[me.z, me.xl, me.k], wo.at[me.z, me.xl, me.k], me.partner(), sends.slot()
     )
 
-    def multiply(step, first=False):
+    def multiply(step, first=False, which=(1, 2, 0)):
         chunk = lax.rem(me.z + 8 + step, 8)
         left = tok[chunk].reshape(512, 512)
-        for j in (1, 2, 0):
+        for j in which:
             part = jnp.dot(left, weights[j, chunk].reshape(512, 256), preferred_element_type=F32)
             if first:
                 acc[j] = part
@@ -393,7 +393,7 @@
     total[...] = jnp.zeros_like(total)
     other_ring.take_ahead(4)
     shared(("a", 4))
-    multiply(4)
+    multiply(4, which=(1, 2))
 
     def finish_projection(j):
         for head in range(2):
@@ -440,6 +440,7 @@
         kv_copy(kv_of(1), 2, plane(3), 1).start()
 
     share(p, kv_of(mine)).start()
+    multiply(4, which=(0,))
     finish_projection(0)
 
     @pl.when(p == 1)
@@ -463,38 +464,50 @@
         return place + core * 256 <= rows + half * 512 + me.k * 256
 
     def pair(slot, b, diagonal):
+        parts = [pl.ds(half * TOK, TOK) for half in range(2)]
+        lengths = [TOK if diagonal and half == 0 else 2 * TOK for half in range(2)]
+        scores = []
         for half in range(2):
-            part = pl.ds(half * TOK, TOK)
-            keys = TOK if diagonal and half == 0 else 2 * TOK
-            q = query[slot, part]
-            scores = []
             for core in range(2):
                 score = lax.dot_general(
-                    q, kv[b, core, 0, pl.ds(0, keys)], (((1,), (1,)), ((), ())), preferred_element_type=F32
+                    query[slot, parts[half]],
+                    kv[b, core, 0, pl.ds(0, lengths[half])],
+                    (((1,), (1,)), ((), ())),
+                    preferred_element_type=F32,
                 ) * scale
                 if diagonal:
-                    score = jnp.where(allowed(half, core, keys), score, -1e30)
+                    score = jnp.where(allowed(half, core, lengths[half]), score, -1e30)
                 scores.append(score)
-            old = top[slot, part]
-            new = jnp.maximum(old, jnp.max(jnp.maximum(scores[0], scores[1]), axis=1, keepdims=True))
-            probs = [jnp.exp(score - new) for score in scores]
-            if diagonal:
-                probs = [
-                    jnp.where(allowed(half, core, keys), probs[core], 0.0) for core in range(2)
-                ]
-            factor = jnp.exp(old - new)
-            top[slot, part] = new
-            denom[slot, part] = denom[slot, part] * factor + jnp.sum(
-                probs[0] + probs[1], axis=1, keepdims=True
-            )
-            result = total[slot, part] * factor
+        olds = [top[slot, part] for part in parts]
+        news, factors, probs = [], [], []
+        for half in range(2):
+            one, two = scores[2 * half : 2 * half + 2]
+            news.append(jnp.maximum(olds[half], jnp.max(jnp.maximum(one, two), axis=1, keepdims=True)))
+            factors.append(jnp.exp(olds[half] - news[half]))
+            for core in range(2):
+                prob = jnp.exp(scores[2 * half + core] - news[half])
+                if diagonal:
+                    prob = jnp.where(allowed(half, core, lengths[half]), prob, 0.0)
+                probs.append(prob)
+        sums = [
+            denom[slot, parts[half]] * factors[half]
+            + jnp.sum(probs[2 * half] + probs[2 * half + 1], axis=1, keepdims=True)
+            for half in range(2)
+        ]
+        results = []
+        for half in range(2):
+            result = total[slot, parts[half]] * factors[half]
             for core in range(2):
                 result = result + jnp.dot(
-                    probs[core].astype(BF16),
-                    kv[b, core, 1, pl.ds(0, keys)],
+                    probs[2 * half + core].astype(BF16),
+                    kv[b, core, 1, pl.ds(0, lengths[half])],
                     preferred_element_type=F32,
                 )
-            total[slot, part] = result
+            results.append(result)
+        for half in range(2):
+            top[slot, parts[half]] = news[half]
+            denom[slot, parts[half]] = sums[half]
+            total[slot, parts[half]] = results[half]
 
     def rows_of(r):
         return pl.ds(pl.multiple_of(r * TOK, TOK), TOK)
@@ -671,7 +684,6 @@
         return merged.at[xh * 4 + y, early + half * (1 - 2 * early)]
 
     gather = HeadGather(sends, me, block_out)
-    ring_b.start()
 
     @pl.when(p == 1)
     def _():
@@ -679,6 +691,7 @@
 
     handed(mine, 1)
     gather.start_a()
+    ring_b.start()
     ring_a.take_ahead(1)
     ring_a.take_back(1)
     handed(1 - mine, 0)

time: 104 us -> 103 us (level)
  no operation moved by 1% of the time
where the time goes in v6:
time: 103 us
  Pallas kernels  101 us (98%)
  local copies, waits for them, and re-layouts  1.67 us (2%)
    pallas_call x1, Pallas kernels, layer(): pl.pallas_call(layer_kernel, out_shape=jax.ShapeDtypeStruct((TOK, 512), B...  101 us

profile of v6, /device:TPU:1, one launch (start us, length us, event | category | flops | bytes accessed | tf_op | source)
XLA Modules:
  0.0 103.1 jit_solution(2593394858935756946)
XLA Ops:
  0.0 101.4 %layer.1 = bf16[256,512]{1,0:T(8,128)(2,1)} custom-call(bf16[256,512]{1,0:T(8,128)(2,1)} %tok_in.1, bf16[128,512]{1,0:T(8,128)(2,1)} %wq_in.1, bf16[128,512]{1,0:T(8,128)(2,1)} %wk_in.1, bf16[128,512]{1,0:T(8,128)(2,1)} %wv_in.1, bf16[128,512]{1,0:T(8,128)(2,1)} %wo_in.1, bf16[24,4096]{1,0:T(8,128)(2,1)} %bitcast.2, bf16[24,512]{1,0:T(8,128)(2,1)} %bitcast.3, ...), custom_call_target="tpu_custom_call" | custom-call | tf_op jit(solution)/shard_map/layer/pallas_call | solution.py:790
  101.4 1.7 %copy.10 = bf16[256,512]{1,0:T(8,128)(2,1)} copy(bf16[256,512]{1,0:T(8,128)(2,1)} %layer.1) | data formatting | bytes 524288
